TPU v7x, 32 devices: a whole 2x2x4 slice. The times are simulated.
32 devices in a mesh: batch: 4 (over z), seq: 8 (over y, x, core).
Axes of the slice: x: 2, y: 2, z: 4, core: 2. Of those that a mesh axis runs over, the one named last changes fastest.
Arguments:
- inputs: float32 [8, 1024, 768], P('batch', 'seq'), may hold values from -6 to 6
- cotangent: float32 [8, 1024, 768], P('batch', 'seq'), may hold values from -6 to 6
- lengths: int32 [8], P('batch'), may hold values from 256 to 1024, as said below
- joint_weight: bfloat16 [768, 2304], P(('batch', 'seq')), may hold values from -0.3125 to 0.3125
- output_weight: bfloat16 [768, 768], P(('batch', 'seq')), may hold values from -1.25 to 1.25
- vectors: bfloat16 [8, 768], P(None, ('batch', 'seq')), may hold values from -2 to 2
- expand_weight: bfloat16 [768, 3072], P(('batch', 'seq')), may hold values from -0.21875 to 0.21875
- expand_bias: bfloat16 [3072], P(('batch', 'seq')), may hold values from -1.1953125 to 1.1953125
- reduce_weight: bfloat16 [3072, 768], P(('batch', 'seq')), may hold values from -0.15625 to 0.15625
Outputs:
- result: float32 [8, 1024, 768], P('batch', 'seq')
- grad_inputs: float32 [8, 1024, 768], P('batch', 'seq')
- grad_joint: float32 [768, 2304], P(('batch', 'seq'))
- grad_output: float32 [768, 768], P(('batch', 'seq'))
- grad_vectors: float32 [8, 768], P(None, ('batch', 'seq'))
- grad_expand: float32 [768, 3072], P(('batch', 'seq'))
- grad_expand_bias: float32 [3072], P(('batch', 'seq'))
- grad_reduce: float32 [3072, 768], P(('batch', 'seq'))
Inputs may be any that keep to these rules, and one draw needn't show every extreme that they name: `lengths`: some sequence is full (1024 valid tokens) in every draw.
All inputs are finite; a program needn't handle non-finite values.
Results may differ from a plain program's by a relative error of at most 0.018.
The roundings to bfloat16 on the way count: a program that leaves them out, or rounds other values in their place, can miss the bound.
Values may be sent and summed in bfloat16 or wider, within the bound.
A program may use at most 192 MiB of HBM per device.

v0:
```python
import functools
import math

import jax
import jax.numpy as jnp
from jax import lax
from jax.experimental import pallas as pl
from jax.experimental.pallas import tpu as pltpu
from jax.sharding import PartitionSpec as P

HEADS = 12
HEAD_DIM = 64


EPSILON = 1e-12
SCORE_SCALE = 0.125
NEG_FILL = -1e30
HALF_ROOT = 0.7071067811865476
INV_ROOT_TAU = 0.3989422804014327
block_limit = 256


def layer_norm(residual, norm_gain, norm_shift):
    centered = residual - jnp.mean(residual, axis=-1, keepdims=True)
    inverse = lax.rsqrt(jnp.mean(centered * centered, axis=-1, keepdims=True) + EPSILON)
    normed = centered * inverse
    return (normed * norm_gain + norm_shift, normed, inverse)


def norm_back(grad_out, normed, inverse, norm_gain):
    grad_normed = grad_out * norm_gain
    mean_grad = jnp.mean(grad_normed, axis=-1, keepdims=True)
    mean_proj = jnp.mean(grad_normed * normed, axis=-1, keepdims=True)
    grad_in = inverse * (grad_normed - mean_grad - normed * mean_proj)
    return (grad_in, jnp.sum(grad_out * normed, axis=0), jnp.sum(grad_out, axis=0))


def gelu_value(before_gelu):
    return 0.5 * before_gelu * (1.0 + lax.erf(before_gelu * HALF_ROOT))


def gelu_slope(before_gelu):
    return (
        0.5 * (1.0 + lax.erf(before_gelu * HALF_ROOT))
        + before_gelu * jnp.exp(-0.5 * before_gelu * before_gelu) * INV_ROOT_TAU
    )


def over_blocks(piece_rows, block_fn, carried):
    block_size = math.gcd(piece_rows, block_limit)

    def run_block(block_index, current):
        return block_fn(current, block_index * block_size, block_size)

    return lax.fori_loop(0, piece_rows // block_size, run_block, carried)


def head_scores(left_heads, right_heads, right_places, lengths):
    scores = (
        jnp.einsum("sqhd,skhd->shqk", left_heads, right_heads, preferred_element_type=jnp.float32)
        * SCORE_SCALE
    )
    allowed = right_places[None, :] < lengths[:, None]
    return jnp.where(allowed[:, None, None, :], scores, NEG_FILL)


def cut_heads(gathered_piece, offset, block_size, head_count):
    sliced = lax.dynamic_slice_in_dim(gathered_piece, offset, block_size, 1)
    return sliced.reshape(sliced.shape[0], block_size, head_count, -1)


def gather_attention(joint_weight, output_weight, vectors):
    return (
        lax.all_gather(joint_weight, ("batch", "seq"), axis=0, tiled=True),
        lax.all_gather(output_weight, ("batch", "seq"), axis=0, tiled=True),
        lax.all_gather(vectors, ("batch", "seq"), axis=1, tiled=True),
    )


def gather_feed(expand_weight, reduce_weight, expand_bias):
    return (
        lax.all_gather(expand_weight, ("batch", "seq"), axis=0, tiled=True),
        lax.all_gather(reduce_weight, ("batch", "seq"), axis=0, tiled=True),
        lax.all_gather(expand_bias, ("batch", "seq"), axis=0, tiled=True),
    )


def general_on_device(
    inputs,
    cotangent,
    lengths,
    joint_weight,
    output_weight,
    vectors,
    expand_weight,
    expand_bias,
    reduce_weight,
):
    seq_count, row_count, model_width = inputs.shape
    head_count = HEADS
    head_size = HEAD_DIM
    tokens = seq_count * row_count
    head_shape = (seq_count, row_count, head_count, head_size)
    own_places = lax.axis_index("seq") * row_count + jnp.arange(row_count, dtype=jnp.int32)
    row_valid = own_places[None, :] < lengths[:, None]
    row_mask = row_valid.reshape(tokens, 1).astype(jnp.float32)
    full_joint, full_output, full_vectors = gather_attention(joint_weight, output_weight, vectors)
    vector_rows = full_vectors.astype(jnp.float32)
    flat_inputs = inputs.reshape(tokens, model_width)
    input_low = flat_inputs.astype(jnp.bfloat16)
    projected = jnp.dot(input_low, full_joint, preferred_element_type=jnp.float32)
    query_low = (projected[:, :model_width] + vector_rows[2]).astype(jnp.bfloat16)
    key_low = projected[:, model_width : 2 * model_width].astype(jnp.bfloat16)
    value_low = (projected[:, 2 * model_width :] + vector_rows[3]).astype(jnp.bfloat16)
    query_heads = query_low.reshape(head_shape)
    key_rows = key_low.reshape(seq_count, row_count, model_width)
    value_rows = value_low.reshape(seq_count, row_count, model_width)
    start_state = (
        jnp.full((seq_count, head_count, row_count), NEG_FILL, jnp.float32),
        jnp.zeros((seq_count, head_count, row_count), jnp.float32),
        jnp.zeros(head_shape, jnp.float32),
    )
    key_piece = lax.all_gather(key_rows, "seq", axis=1, tiled=True)
    value_piece = lax.all_gather(value_rows, "seq", axis=1, tiled=True)

    def forward_score_block(current, offset, block_size):
        running_max, running_sum, summed = current
        key_heads = cut_heads(key_piece, offset, block_size, head_count)
        value_heads = cut_heads(value_piece, offset, block_size, head_count)
        key_places = offset + jnp.arange(block_size, dtype=jnp.int32)
        scores = head_scores(query_heads, key_heads, key_places, lengths)
        new_max = jnp.maximum(running_max, jnp.max(scores, axis=-1))
        factor = jnp.exp(running_max - new_max)
        exp_scores = jnp.exp(scores - new_max[..., None])
        running_sum = running_sum * factor + jnp.sum(exp_scores, axis=-1)
        update = jnp.einsum(
            "shqk,skhd->sqhd",
            exp_scores.astype(jnp.bfloat16),
            value_heads,
            preferred_element_type=jnp.float32,
        )
        summed = summed * jnp.transpose(factor, (0, 2, 1))[..., None] + update
        return (new_max, running_sum, summed)

    running_max, running_sum, summed = over_blocks(
        key_piece.shape[1], forward_score_block, start_state
    )
    attended = summed / jnp.transpose(running_sum, (0, 2, 1))[..., None]
    log_total = jnp.transpose(running_max + jnp.log(running_sum), (0, 2, 1))
    context_low = attended.reshape(tokens, model_width).astype(jnp.bfloat16)
    branch = jnp.dot(context_low, full_output, preferred_element_type=jnp.float32) + vector_rows[4]
    first, first_normed, first_inverse = layer_norm(
        flat_inputs + branch, vector_rows[0], vector_rows[1]
    )
    first_low = first.astype(jnp.bfloat16)
    full_expand, full_reduce, full_bias = gather_feed(expand_weight, reduce_weight, expand_bias)
    before_gelu = jnp.dot(
        first_low, full_expand, preferred_element_type=jnp.float32
    ) + full_bias.astype(jnp.float32)
    hidden_low = gelu_value(before_gelu).astype(jnp.bfloat16)
    feed = jnp.dot(hidden_low, full_reduce, preferred_element_type=jnp.float32) + vector_rows[7]
    result, second_normed, second_inverse = layer_norm(first + feed, vector_rows[5], vector_rows[6])
    full_expand, full_reduce, full_bias = gather_feed(expand_weight, reduce_weight, expand_bias)
    full_joint, full_output, full_vectors = gather_attention(joint_weight, output_weight, vectors)
    grad_res = cotangent.reshape(tokens, model_width) * row_mask
    grad_second, grad_gain_two, grad_shift_two = norm_back(
        grad_res, second_normed, second_inverse, vector_rows[5]
    )
    grad_feed_low = grad_second.astype(jnp.bfloat16)
    grad_reduce_local = jnp.dot(hidden_low.T, grad_feed_low, preferred_element_type=jnp.float32)
    grad_hidden = jnp.dot(
        grad_feed_low, full_reduce.T, preferred_element_type=jnp.float32
    ) * gelu_slope(before_gelu)
    grad_hidden_low = grad_hidden.astype(jnp.bfloat16)
    grad_expand_local = jnp.dot(first_low.T, grad_hidden_low, preferred_element_type=jnp.float32)
    grad_bias_local = jnp.sum(grad_hidden_low.astype(jnp.float32), axis=0)
    grad_first = grad_second + jnp.dot(
        grad_hidden_low, full_expand.T, preferred_element_type=jnp.float32
    )
    grad_resid, grad_gain_one, grad_shift_one = norm_back(
        grad_first, first_normed, first_inverse, vector_rows[0]
    )
    grad_branch_low = grad_resid.astype(jnp.bfloat16)
    grad_output_local = jnp.dot(context_low.T, grad_branch_low, preferred_element_type=jnp.float32)
    grad_context_low = jnp.dot(
        grad_branch_low, full_output.T, preferred_element_type=jnp.float32
    ).astype(jnp.bfloat16)
    grad_context_heads = grad_context_low.reshape(head_shape)
    row_delta = jnp.sum(grad_context_heads.astype(jnp.float32) * attended, axis=-1)
    log_heads = jnp.transpose(log_total, (0, 2, 1))
    delta_heads = jnp.transpose(row_delta, (0, 2, 1))
    query_key_piece = lax.all_gather(key_rows, "seq", axis=1, tiled=True)
    query_value_piece = lax.all_gather(value_rows, "seq", axis=1, tiled=True)

    def query_score_block(current, offset, block_size):
        key_heads = cut_heads(query_key_piece, offset, block_size, head_count)
        value_heads = cut_heads(query_value_piece, offset, block_size, head_count)
        key_places = offset + jnp.arange(block_size, dtype=jnp.int32)
        scores = head_scores(query_heads, key_heads, key_places, lengths)
        softmax_rows = jnp.exp(scores - log_heads[..., None])
        grad_probs = jnp.einsum(
            "sqhd,skhd->shqk", grad_context_heads, value_heads, preferred_element_type=jnp.float32
        )
        grad_scores = (softmax_rows * (grad_probs - delta_heads[..., None])).astype(jnp.bfloat16)
        return (
            current
            + jnp.einsum(
                "shqk,skhd->sqhd", grad_scores, key_heads, preferred_element_type=jnp.float32
            )
            * SCORE_SCALE
        )

    grad_query = over_blocks(
        query_key_piece.shape[1], query_score_block, jnp.zeros(head_shape, jnp.float32)
    )
    own_keys = key_low.reshape(head_shape)
    own_values = value_low.reshape(head_shape)
    query_rows = query_low.reshape(seq_count, row_count, model_width)
    grad_context_rows = grad_context_low.reshape(seq_count, row_count, model_width)
    zero_heads = jnp.zeros(head_shape, jnp.float32)
    query_piece = lax.all_gather(query_rows.astype(jnp.float32), "seq", axis=1, tiled=True).astype(
        jnp.bfloat16
    )
    grad_piece = lax.all_gather(
        grad_context_rows.astype(jnp.float32), "seq", axis=1, tiled=True
    ).astype(jnp.bfloat16)
    log_piece = lax.all_gather(log_total, "seq", axis=1, tiled=True)
    delta_piece = lax.all_gather(row_delta, "seq", axis=1, tiled=True)

    def key_score_block(current, offset, block_size):
        grad_key, grad_value = current
        query_block = cut_heads(query_piece, offset, block_size, head_count)
        grad_block = cut_heads(grad_piece, offset, block_size, head_count)
        log_block = jnp.transpose(
            lax.dynamic_slice_in_dim(log_piece, offset, block_size, 1), (0, 2, 1)
        )
        delta_block = jnp.transpose(
            lax.dynamic_slice_in_dim(delta_piece, offset, block_size, 1), (0, 2, 1)
        )
        scores = head_scores(query_block, own_keys, own_places, lengths)
        softmax_rows = jnp.exp(scores - log_block[..., None])
        grad_value = grad_value + jnp.einsum(
            "shqk,sqhd->skhd",
            softmax_rows.astype(jnp.bfloat16),
            grad_block,
            preferred_element_type=jnp.float32,
        )
        grad_probs = jnp.einsum(
            "sqhd,skhd->shqk", grad_block, own_values, preferred_element_type=jnp.float32
        )
        grad_scores = (softmax_rows * (grad_probs - delta_block[..., None])).astype(jnp.bfloat16)
        grad_key = (
            grad_key
            + jnp.einsum(
                "shqk,sqhd->skhd", grad_scores, query_block, preferred_element_type=jnp.float32
            )
            * SCORE_SCALE
        )
        return (grad_key, grad_value)

    grad_key, grad_value = over_blocks(
        query_piece.shape[1], key_score_block, (zero_heads, zero_heads)
    )
    grad_query_low = grad_query.reshape(tokens, model_width).astype(jnp.bfloat16)
    grad_key_low = grad_key.reshape(tokens, model_width).astype(jnp.bfloat16)
    grad_value_low = grad_value.reshape(tokens, model_width).astype(jnp.bfloat16)
    grad_projected = jnp.concatenate([grad_query_low, grad_key_low, grad_value_low], axis=1)
    grad_joint_local = jnp.dot(input_low.T, grad_projected, preferred_element_type=jnp.float32)
    grad_inputs = grad_resid + jnp.dot(
        grad_projected, full_joint.T, preferred_element_type=jnp.float32
    )
    grad_vector_local = jnp.stack(
        [
            grad_gain_one,
            grad_shift_one,
            jnp.sum(grad_query_low.astype(jnp.float32), axis=0),
            jnp.sum(grad_value_low.astype(jnp.float32), axis=0),
            jnp.sum(grad_branch_low.astype(jnp.float32), axis=0),
            grad_gain_two,
            grad_shift_two,
            jnp.sum(grad_feed_low.astype(jnp.float32), axis=0),
        ],
        axis=0,
    )
    every_grad = (
        lax.psum_scatter(grad_joint_local, ("batch", "seq"), scatter_dimension=0, tiled=True),
        lax.psum_scatter(grad_output_local, ("batch", "seq"), scatter_dimension=0, tiled=True),
        lax.psum_scatter(grad_vector_local, ("batch", "seq"), scatter_dimension=1, tiled=True),
        lax.psum_scatter(grad_expand_local, ("batch", "seq"), scatter_dimension=0, tiled=True),
        lax.psum_scatter(grad_reduce_local, ("batch", "seq"), scatter_dimension=0, tiled=True),
        lax.psum_scatter(grad_bias_local, ("batch", "seq"), scatter_dimension=0, tiled=True),
    )
    summed_grads = (
        every_grad[0],
        every_grad[1],
        every_grad[2],
        every_grad[3],
        every_grad[5],
        every_grad[4],
    )
    return (
        result.reshape(seq_count, row_count, model_width),
        grad_inputs.reshape(seq_count, row_count, model_width),
        summed_grads[0],
        summed_grads[1],
        summed_grads[2],
        summed_grads[3],
        summed_grads[4],
        summed_grads[5],
    )


MESH = pl.DeviceIdType.MESH
ANY = pl.BlockSpec(memory_space=pl.ANY)
VM = pl.BlockSpec(memory_space=pltpu.VMEM)
SM = pl.BlockSpec(memory_space=pltpu.SMEM)
DMA = pltpu.SemaphoreType.DMA
VMEM_LIMIT = 60 << 20
F32 = jnp.float32
BF16 = jnp.bfloat16


def send(src, dst, send_sem, recv_sem, device):
    return pltpu.make_async_remote_copy(
        src_ref=src,
        dst_ref=dst,
        send_sem=send_sem,
        recv_sem=recv_sem,
        device_id=device,
        device_id_type=MESH,
    )


class Place:
    def __init__(self, nb):
        self.nb = nb
        self.b = lax.axis_index("batch")
        self.s = lax.axis_index("seq")
        self.c = self.s % 2
        self.p = self.s // 2
        x, y = self.p % 2, self.p // 2
        self.px = 2 * y + (1 - x)
        self.py = 2 * (1 - y) + x
        self.pd = 2 * (1 - y) + (1 - x)
        self.sib = (self.b, 2 * self.p + 1 - self.c)
        self.xn = (self.b, 2 * self.px + self.c)
        self.yn = (self.b, 2 * self.py + self.c)

    def chip(self, step):
        return (self.p, self.px, self.py, self.pd)[step]

    def up(self, step):
        return (self.b + step) % self.nb

    def down(self, step):
        return (self.b + self.nb - step) % self.nb


def greet_near(pos):
    barrier = pltpu.get_barrier_semaphore()

    def signal(device):
        pl.semaphore_signal(barrier, inc=1, device_id=device, device_id_type=MESH)

    for device in plane_others(pos):
        signal(device)
    last = pos.nb - 1
    guarded(pos.b < last, lambda: signal(((pos.b + 1) % pos.nb, pos.s)))
    guarded(pos.b > 0, lambda: signal(((pos.b + last) % pos.nb, pos.s)))
    beside = jnp.where(pos.b < last, 1, 0) + jnp.where(pos.b > 0, 1, 0)
    pl.semaphore_wait(barrier, 7 + beside)


def same_core(pos):
    return [
        (pos.up(d), 2 * pos.chip(k) + pos.c)
        for d in range(pos.nb)
        for k in range(4)
        if d or k
    ]


def plane_others(pos):
    return [
        (pos.b, 2 * pos.chip(k) + (pos.c if j == 0 else 1 - pos.c))
        for k in range(4)
        for j in range(2)
        if k or j
    ]


def guarded(condition, action):
    if isinstance(condition, bool):
        if condition:
            action()
    else:

        @pl.when(condition)
        def _():
            action()


class Chain:
    def __init__(self, pos, mine, spot, sems):
        self.pos, self.mine, self.spot = pos, mine, spot
        self.up, self.down = sems

    @staticmethod
    def scratch(nb):
        return [DMA((2, nb)), DMA((2, nb))]

    def copy(self, src, z, sems, hop, there):
        pos = self.pos
        return send(src, self.spot(z), sems.at[0, hop], sems.at[1, hop], (there, pos.s))

    def moves(self, hop):
        pos = self.pos
        last = pos.nb - 1
        low, high = (pos.b - hop + 1 + pos.nb) % pos.nb, (pos.b + hop - 1) % pos.nb
        above, below = (pos.b + 1) % pos.nb, (pos.b + last) % pos.nb
        own = isinstance(hop, int) and hop == 1
        return (
            (
                (pos.b >= hop - 1) & (pos.b < last),
                self.copy(self.mine if own else self.spot(low), low, self.up, hop, above),
            ),
            (
                (pos.b + hop - 1 < pos.nb) & (pos.b > 0),
                self.copy(self.mine if own else self.spot(high), high, self.down, hop, below),
            ),
        )

    def start(self, hop=1):
        for made, copy in self.moves(hop):
            guarded(made, copy.start)

    def hop(self, hop):
        pos = self.pos
        low, high = (pos.b - hop + pos.nb) % pos.nb, (pos.b + hop) % pos.nb
        for made, z, sems in (
            (pos.b >= hop, low, self.up),
            (pos.b + hop < pos.nb, high, self.down),
        ):
            guarded(made, self.copy(self.spot(z), z, sems, hop, pos.b).wait_recv)
        guarded(hop < pos.nb - 1, lambda: self.start(hop + 1))

    def drain(self):
        for hop in range(1, self.pos.nb):
            for made, copy in self.moves(hop):
                guarded(made, copy.wait_send)


class Gather:
    def __init__(self, pos, shard, out, halves, tall, sems):
        self.tall = tall
        self.pos, self.shard, self.out, self.halves = pos, shard, out, halves
        self.xs, self.ys, self.f0, self.f1, self.sb, self.local_sem = sems[:6]
        self.chain = Chain(pos, shard, lambda z: out.at[z, pos.p, pos.c], sems[6:8])
        self.across = Chain(
            pos, out.at[pos.b, pos.pd, pos.c], lambda z: out.at[z, pos.pd, pos.c], sems[8:]
        )

    @staticmethod
    def scratch(nb):
        return [DMA((2, nb))] * 5 + [DMA] + Chain.scratch(nb) * 2

    def z(self, k):
        return jnp.where(k <= self.pos.b, self.pos.b - k, k)

    def own(self):
        pos = self.pos
        self.local = pltpu.make_async_copy(
            self.shard, self.out.at[pos.b, pos.p, pos.c], self.local_sem
        )
        self.local.start()

    def x_copy(self, k, src=None):
        pos = self.pos
        there = self.out.at[self.z(k), pos.p, pos.c]
        src = there if src is None else src
        return send(src, there, self.xs.at[0, k], self.xs.at[1, k], pos.xn)

    def y_copy(self, k, src=None):
        pos = self.pos
        there = self.out.at[self.z(k), pos.p, pos.c]
        src = there if src is None else src
        return send(src, there, self.ys.at[0, k], self.ys.at[1, k], pos.yn)

    def plane(self, k, src=None):
        self.x_copy(k, src).start()
        self.y_copy(k, src).start()

    def landed(self, sems, k, chip):
        pos = self.pos
        ref = self.out.at[self.z(k), chip, pos.c]
        send(ref, ref, sems.at[0, k], sems.at[1, k], pos.xn).wait_recv()

    def y_forward(self, k):
        pos = self.pos
        ref = self.out.at[self.z(k), pos.px, pos.c].at[self.halves[0]]
        return send(ref, ref, self.f0.at[0, k], self.f0.at[1, k], pos.yn)

    def x_forward(self, k):
        pos = self.pos
        ref = self.out.at[self.z(k), pos.py, pos.c].at[self.halves[1]]
        return send(ref, ref, self.f1.at[0, k], self.f1.at[1, k], pos.xn)

    def two_ways(self, k):
        return True if not self.tall else k == 0

    def forward(self, k):
        pos = self.pos
        self.landed(self.xs, k, pos.px)
        guarded(self.two_ways(k), lambda: self.y_forward(k).start())
        self.landed(self.ys, k, pos.py)
        if self.halves[1] is not None:
            guarded(self.two_ways(k), lambda: self.x_forward(k).start())

    def crossed(self, k):
        pos = self.pos
        across = self.out.at[self.z(k), pos.pd, pos.c]
        for half, sems in zip(self.halves, (self.f0, self.f1)):
            if half is not None:
                ref = across.at[half]
                send(ref, ref, sems.at[0, k], sems.at[1, k], pos.xn).wait_recv()

    def complete(self, k):
        if not self.tall:
            self.crossed(k)
        elif isinstance(k, int) and k == 0:
            self.crossed(k)
            self.across.start()
        else:
            self.across.hop(k)

    def sibling_copy(self, k):
        pos = self.pos
        ref = self.out.at[self.z(k), :, pos.c]
        return send(ref, ref, self.sb.at[0, k], self.sb.at[1, k], pos.sib)

    def sibling(self, k):
        self.sibling_copy(k).start()

    def finish(self, k):
        pos = self.pos
        ref = self.out.at[self.z(k), :, 1 - pos.c]
        send(ref, ref, self.sb.at[0, k], self.sb.at[1, k], pos.sib).wait_recv()
        self.x_copy(k).wait_send()
        self.y_copy(k).wait_send()
        self.sibling_copy(k).wait_send()
        guarded(self.two_ways(k), lambda: self.y_forward(k).wait_send())
        if self.halves[1] is not None:
            guarded(self.two_ways(k), lambda: self.x_forward(k).wait_send())

    def drain(self):
        self.chain.drain()
        if self.tall:
            self.across.drain()


class InputExchange:
    def __init__(self, pos, rows, out, sems):
        self.pos, self.rows, self.out, self.sems = pos, rows, out, sems
        self.started = []

    @staticmethod
    def scratch():
        return [DMA((2, 2)), DMA((2, 2)), DMA((2, 2)), DMA((2,)), DMA]

    def go(self, copy):
        copy.start()
        self.started.append(copy)

    def start(self):
        pos, (xs, ys, _, sb, local) = self.pos, self.sems
        there = self.out.at[pos.p, pos.c]
        for sems, chip in ((xs, pos.px), (ys, pos.py)):
            for j in range(2):
                self.go(
                    send(
                        self.rows.at[j],
                        there,
                        sems.at[0, j],
                        sems.at[1, pos.c],
                        (pos.b, 2 * chip + j),
                    )
                )
        self.go(send(self.rows.at[1 - pos.c], there, sb.at[0], sb.at[1], pos.sib))
        self.local = pltpu.make_async_copy(self.rows.at[pos.c], there, local)
        self.local.start()

    def landed(self, sems, j, chip):
        ref = self.out.at[chip, j]
        send(ref, ref, sems.at[0, j], sems.at[1, j], self.pos.xn).wait_recv()

    def forward(self):
        pos, (xs, ys, fs, _, _) = self.pos, self.sems
        self.landed(xs, 0, pos.px)
        ref = self.out.at[pos.px, 0]
        self.go(send(ref, ref, fs.at[0, 0], fs.at[1, 0], pos.yn))
        self.landed(ys, 1, pos.py)
        ref = self.out.at[pos.py, 1]
        self.go(send(ref, ref, fs.at[0, 1], fs.at[1, 1], pos.xn))

    def finish(self):
        pos, (xs, ys, fs, sb, _) = self.pos, self.sems
        self.landed(xs, 1, pos.px)
        self.landed(ys, 0, pos.py)
        self.landed(fs, 0, pos.pd)
        self.landed(fs, 1, pos.pd)
        ref = self.out.at[pos.p, 1 - pos.c]
        send(ref, ref, sb.at[0], sb.at[1], pos.sib).wait_recv()
        self.local.wait()

    def drain(self):
        for copy in self.started:
            copy.wait_send()


class JointGather:
    def __init__(self, pos, parts, out, sems):
        self.pos, self.parts, self.out = pos, parts, out
        self.direct, self.sb, self.local_sem = sems[:3]
        self.chain = Chain(
            pos, out.at[pos.b, :, pos.c], lambda z: out.at[z, :, pos.c], sems[3:]
        )

    @staticmethod
    def scratch(nb):
        return [DMA((2, 4)), DMA((2,)), DMA] + Chain.scratch(nb)

    def start(self):
        pos = self.pos
        there = self.out.at[pos.b, pos.p, pos.c]
        self.started = [
            send(
                self.parts.at[pos.chip(k)],
                there,
                self.direct.at[0, k],
                self.direct.at[1, k],
                (pos.b, 2 * pos.chip(k) + pos.c),
            )
            for k in range(1, 4)
        ]
        for copy in self.started:
            copy.start()
        self.local = pltpu.make_async_copy(self.parts.at[pos.p], there, self.local_sem)
        self.local.start()

    def own(self):
        pos = self.pos
        for k in range(1, 4):
            ref = self.out.at[pos.b, pos.chip(k), pos.c]
            send(ref, ref, self.direct.at[0, k], self.direct.at[1, k], pos.sib).wait_recv()
        self.local.wait()
        self.chain.start()

    def sibling(self):
        pos = self.pos
        ref = self.out.at[:, :, pos.c]
        send(ref, ref, self.sb.at[0], self.sb.at[1], pos.sib).start()

    def finish(self):
        pos = self.pos
        ref = self.out.at[:, :, 1 - pos.c]
        send(ref, ref, self.sb.at[0], self.sb.at[1], pos.sib).wait_recv()

    def drain(self):
        for copy in self.started:
            copy.wait_send()
        ref = self.out.at[:, :, self.pos.c]
        send(ref, ref, self.sb.at[0], self.sb.at[1], self.pos.sib).wait_send()
        self.chain.drain()


class ContextExchange:
    def __init__(self, pos, parts, out, sems):
        self.pos, self.parts, self.out = pos, parts, out
        self.sems, self.local_sem = sems

    @staticmethod
    def scratch():
        return [DMA((2, 8)), DMA]

    def pairs(self):
        pos = self.pos
        for k in range(4):
            for j in range(2):
                if k or j:
                    yield 2 * k + j, pos.chip(k), pos.c if j == 0 else 1 - pos.c

    def copies(self):
        pos, sems = self.pos, self.sems
        there = self.out.at[pos.p, pos.c]
        return [
            send(
                self.parts.at[chip, core],
                there,
                sems.at[0, i],
                sems.at[1, i],
                (pos.b, 2 * chip + core),
            )
            for i, chip, core in self.pairs()
        ]

    def local(self):
        pos = self.pos
        return pltpu.make_async_copy(
            self.parts.at[pos.p, pos.c], self.out.at[pos.p, pos.c], self.local_sem
        )

    def start(self):
        for copy in self.copies():
            copy.start()
        self.local().start()

    def arrive(self):
        for i, chip, core in self.pairs():
            ref = self.out.at[chip, core]
            send(ref, ref, self.sems.at[0, i], self.sems.at[1, i], self.pos.sib).wait_recv()
        self.local().wait()

    def drain(self):
        for copy in self.copies():
            copy.wait_send()


def gather_attend(
    lengths, inputs, joint, vectors, hidden_bias, output, expand, reduce, nb, heads
):
    _, count, model_width = inputs.shape
    shard = vec = model_width // (8 * nb)
    per = reduce.shape[0]
    width = heads * HEAD_DIM
    size = 8 * count
    joint_shape = (4, shard, 3 * width + 64)
    small_shape = (16, 128)

    def body(
        lengths_ref, inputs_ref, joint_weight_ref, own_vectors_ref, own_bias_ref,
        output_ref, expand_ref, reduce_ref,
        vectors_out, hidden_out, rows_any, weight_any, qkv_any, log_any,
        context_out, output_out, expand_out, reduce_out,
        rows_out, weight_out, qkv_out, log_out, stores,
        joint_all, context, small_all, bias_ref, rows_ref, joint_ref, small_ref,
        *scratch,
    ):
        pos = Place(nb)
        scratch = list(scratch)

        def take(n):
            got = scratch[:n]
            del scratch[:n]
            return got

        exchange = InputExchange(pos, rows_ref, rows_out, take(5))
        joints = JointGather(pos, joint_ref, joint_all, take(5))
        mixing = ContextExchange(pos, context, context_out, take(2))
        outputs, expands, reduces, smalls = (
            Gather(pos, part, out, halves_of(part.shape), tall, take(10))
            for part, out, tall in (
                (output_ref, output_out, True),
                (expand_ref, expand_out, True),
                (reduce_ref, reduce_out, True),
                (small_ref, small_all, True),
            )
        )
        gathers = (expands, smalls, reduces, outputs)
        units = ((expands, smalls), (reduces,), (outputs,))

        saves = [
            pltpu.make_async_copy(src, dst, stores.at[n])
            for n, (src, dst) in enumerate(
                (
                    (rows_out, rows_any),
                    (weight_out, weight_any),
                    (qkv_out, qkv_any),
                    (log_out, log_any),
                )
            )
        ]

        def project(i, _):
            at = pl.ds(pl.multiple_of(i * 2 * count, 2 * count), 2 * count)
            qkv_out[at, :] = (
                jnp.dot(
                    rows_out[i].reshape(2 * count, model_width),
                    weight_out[...],
                    preferred_element_type=F32,
                )
                + bias_ref[...]
            ).astype(BF16)
            return 0

        def prepare():
            joints.finish()
            for z in range(nb):
                weight_out[z * 8 * shard : (z + 1) * 8 * shard, :] = joint_all[
                    z, :, :, :, : 3 * width
                ].reshape(8 * shard, 3 * width)
            bias_ref[...] = jnp.zeros_like(bias_ref)
            for s in range(8):
                spot = joint_all[pos.p, s // 2, s % 2, :, 3 * width :].astype(F32)
                bias_ref[:, s * vec : (s + 1) * vec] = spot[0:1, :vec]
                bias_ref[:, 2 * width + s * vec : 2 * width + (s + 1) * vec] = spot[1:2, :vec]
            lax.fori_loop(0, 4, project, 0)
            for copy in saves[:3]:
                copy.start()

        def hop(k):
            for gather in gathers:
                gather.chain.hop(k)

        def hand_on(k, some):
            for gather in some:
                gather.complete(k)
            for gather in some:
                if k:
                    gather.forward(k)
                gather.sibling(k)

        attend = attend_block(lengths_ref[pos.c], qkv_out, log_out, context, heads, count)

        def spread(k):
            for gather in gathers:
                gather.plane(k)

        weight = joint_weight_ref[...]
        spot = jnp.pad(
            own_vectors_ref[2:4, :].astype(F32), ((0, shard - 2), (0, 64 - vec))
        ).astype(BF16)
        for chip in range(4):
            at = slice(chip * width, (chip + 1) * width)
            joint_ref[chip] = jnp.concatenate(
                [weight[:, n * model_width :][:, at] for n in range(3)] + [spot], axis=1
            )
        small_ref[...] = jnp.concatenate(
            [
                jnp.pad(own_vectors_ref[...].astype(F32), ((0, 0), (0, 128 - vec))),
                jnp.pad(own_bias_ref[...].astype(F32), ((0, 7), (0, 128 - per))),
            ]
        ).astype(BF16)
        rows_ref[...] = inputs_ref[...].astype(BF16)
        greet_near(pos)
        joints.start()
        for gather in gathers:
            gather.own()
            gather.chain.start()
            gather.plane(0, gather.shard)
        joints.own()
        for n, gather in enumerate(gathers):
            gather.local.wait()
            gather.forward(0)
            if n == 1:
                exchange.start()
        hop(1)
        joints.chain.hop(1)
        hand_on(0, gathers)
        spread(1)
        joints.chain.hop(2)
        hop(2)
        exchange.forward()
        joints.chain.hop(3)
        joints.sibling()
        hop(3)
        for gather in units[0]:
            gather.plane(2)
        exchange.finish()
        for unit in units[1:]:
            for gather in unit:
                gather.plane(2)
        spread(3)
        prepare()
        hand_on(1, gathers)
        for i in range(3):
            attend(i)
        hand_on(2, gathers)
        attend(3)
        mixing.start()
        saves[3].start()
        hand_on(nb - 1, (smalls,))

        def finish(some):
            def done(k, _):
                for gather in some:
                    gather.finish(k)
                return 0

            return done

        lax.fori_loop(0, nb, finish((smalls,)), 0)
        for owner in range(8 * nb):
            part = small_all[owner // 8, owner % 8 // 2, owner % 2].astype(F32)
            vectors_out[:, owner * vec : (owner + 1) * vec] = part[:8, :vec]
            hidden_out[:, owner * per : (owner + 1) * per] = part[8:9, :per]
        large = (expands, reduces, outputs)
        lax.fori_loop(0, nb - 1, finish(large), 0)
        smalls.drain()
        mixing.arrive()
        exchange.drain()
        joints.drain()
        mixing.drain()
        hand_on(nb - 1, large)
        for gather in large:
            gather.drain()
        finish(large)(nb - 1, 0)
        for copy in saves:
            copy.wait()

    kept = (
        ((4, 2) + inputs.shape[1:], BF16),
        ((model_width, 3 * width), BF16),
        ((size, 3 * width), BF16),
        ((size, 128), F32),
    )

    def shape(part):
        return jax.ShapeDtypeStruct((nb, 4, 2) + part.shape, part.dtype)

    return pl.pallas_call(
        body,
        out_shape=(
            jax.ShapeDtypeStruct((8, model_width), F32),
            jax.ShapeDtypeStruct((1, 8 * nb * per), F32),
            *(jax.ShapeDtypeStruct(shape, dtype) for shape, dtype in kept),
            jax.ShapeDtypeStruct((4, 2, count, width), BF16),
            shape(output),
            shape(expand),
            shape(reduce),
        ),
        in_specs=[SM] + [VM] * 7,
        out_specs=(VM,) * 2 + (ANY,) * 8,
        scratch_shapes=[pltpu.VMEM(shape, dtype) for shape, dtype in kept]
        + [DMA((4,))]
        + [
            pltpu.VMEM((nb, 4, 2) + joint_shape[1:], BF16),
            pltpu.VMEM((4, 2, count, width), BF16),
            pltpu.VMEM((nb, 4, 2) + small_shape, BF16),
            pltpu.VMEM((1, 3 * width), F32),
            pltpu.VMEM(inputs.shape, BF16),
            pltpu.VMEM(joint_shape, BF16),
            pltpu.VMEM(small_shape, BF16),
        ]
        + InputExchange.scratch()
        + JointGather.scratch(nb)
        + ContextExchange.scratch()
        + Gather.scratch(nb) * 4,
        name="gather_attend",
        compiler_params=pltpu.CompilerParams(
            collective_id=1, has_side_effects=True, vmem_limit_bytes=VMEM_LIMIT
        ),
    )(lengths, inputs, joint, vectors, hidden_bias, output, expand, reduce)


def halves_of(shape):
    rows, columns = shape
    if columns % 256 == 0 and columns >= 1024:
        return (
            (slice(None), pl.ds(0, columns // 2)),
            (slice(None), pl.ds(columns // 2, columns // 2)),
        )
    if rows % 32 == 0:
        return (
            (pl.ds(0, rows // 2), slice(None)),
            (pl.ds(rows // 2, rows // 2), slice(None)),
        )
    if columns % 256 == 0:
        return (
            (slice(None), pl.ds(0, columns // 2)),
            (slice(None), pl.ds(columns // 2, columns // 2)),
        )
    return ((slice(None), slice(None)), None)


def attend_block(limit, qkv_ref, log_ref, context_ref, heads, count):
    width = heads * HEAD_DIM
    size = 8 * count

    def part(n, _):
        at = pl.ds(pl.multiple_of(n * count, count), count)
        allowed = lax.broadcasted_iota(jnp.int32, (1, size), 1) < limit
        lanes = lax.broadcasted_iota(jnp.int32, (count, 128), 1)
        parts, logs = [], jnp.zeros((count, 128), F32)
        for h in range(heads):
            query = qkv_ref[at, h * HEAD_DIM : (h + 1) * HEAD_DIM]
            key = qkv_ref[:, width + h * HEAD_DIM : width + (h + 1) * HEAD_DIM]
            value = qkv_ref[:, 2 * width + h * HEAD_DIM : 2 * width + (h + 1) * HEAD_DIM]
            scores = (
                lax.dot_general(
                    query, key, (((1,), (1,)), ((), ())), preferred_element_type=F32
                )
                * SCORE_SCALE
            )
            scores = jnp.where(allowed, scores, NEG_FILL)
            top = jnp.max(scores, axis=-1, keepdims=True)
            exps = jnp.exp(scores - top)
            total = jnp.sum(exps, axis=-1, keepdims=True)
            mixed = jnp.dot(exps.astype(BF16), value, preferred_element_type=F32)
            parts.append(mixed / total)
            logs = jnp.where(lanes == h, top + jnp.log(total), logs)
        context_ref[n // 2, n % 2] = jnp.concatenate(parts, axis=1).astype(BF16)
        log_ref[at, :] = logs
        return 0

    def block(i):
        lax.fori_loop(2 * i, 2 * i + 2, part, 0)

    return block


def attend_back_block(limit, qkv_ref, log_ref, grad_ref, grad_qkv, grad_key, grad_value, heads, count):
    width = heads * HEAD_DIM
    size = 8 * count
    along_keys = (((1,), (1,)), ((), ()))
    along_rows = (((0,), (0,)), ((), ()))

    def part(n, _):
        at = pl.ds(pl.multiple_of(n * count, count), count)
        allowed = lax.broadcasted_iota(jnp.int32, (1, size), 1) < limit
        grads = grad_ref[n // 2, n % 2]
        parts = []
        for h in range(heads):
            query = qkv_ref[at, h * HEAD_DIM : (h + 1) * HEAD_DIM]
            key = qkv_ref[:, width + h * HEAD_DIM : width + (h + 1) * HEAD_DIM]
            value = qkv_ref[:, 2 * width + h * HEAD_DIM : 2 * width + (h + 1) * HEAD_DIM]
            grad_out = grads[:, h * HEAD_DIM : (h + 1) * HEAD_DIM]
            scores = (
                lax.dot_general(query, key, along_keys, preferred_element_type=F32)
                * SCORE_SCALE
            )
            probs = jnp.where(allowed, jnp.exp(scores - log_ref[at, h : h + 1]), 0.0)
            grad_probs = lax.dot_general(
                grad_out, value, along_keys, preferred_element_type=F32
            )
            delta = jnp.sum(probs * grad_probs, axis=-1, keepdims=True)
            grad_scores = (probs * (grad_probs - delta)).astype(BF16)
            parts.append(
                jnp.dot(grad_scores, key, preferred_element_type=F32) * SCORE_SCALE
            )
            key_part = lax.dot_general(
                grad_scores, query, along_rows, preferred_element_type=F32
            )
            value_part = lax.dot_general(
                probs.astype(BF16), grad_out, along_rows, preferred_element_type=F32
            )
            own = slice(h * HEAD_DIM, (h + 1) * HEAD_DIM)
            grad_key[:, own] += key_part
            grad_value[:, own] += value_part
        grad_qkv[at, :width] = jnp.concatenate(parts, axis=1).astype(BF16)
        return 0

    def block(i):
        lax.fori_loop(2 * i, 2 * i + 2, part, 0)

    return block


class Scatter:
    def __init__(self, pos, halves, bufs, sems):
        self.pos, self.halves = pos, halves
        (self.partial, self.theirs, self.a0, self.a1, self.bx, self.by, self.z) = bufs
        (self.sb, self.s0, self.s1, self.dx, self.dy, self.cx, self.cy, self.zs) = sems

    @staticmethod
    def scratch(nb, shape, dtype, halves):
        first, second = half_shapes(shape, halves)
        return [
            pltpu.VMEM((nb, 4, 2) + shape, dtype),
            pltpu.VMEM((nb, 4) + shape, dtype),
            pltpu.VMEM((nb,) + first, dtype),
            pltpu.VMEM((nb,) + second, dtype),
            pltpu.VMEM((nb,) + shape, dtype),
            pltpu.VMEM((nb,) + shape, dtype),
            pltpu.VMEM((nb,) + shape, dtype),
        ]

    @staticmethod
    def sem_scratch(nb):
        return [DMA((2, nb)) for _ in range(8)]

    def mine(self, k, chip):
        return self.partial.at[self.pos.up(k), chip, self.pos.c]

    def sibling_copy(self, k):
        pos = self.pos
        z = pos.up(k)
        return send(
            self.partial.at[z, :, 1 - pos.c],
            self.theirs.at[z],
            self.sb.at[0, k],
            self.sb.at[1, k],
            pos.sib,
        )

    def begin(self, k):
        self.sibling_copy(k).start()

    def copy(self, k, src, dst, sems, there):
        return send(src, dst, sems.at[0, k], sems.at[1, k], there)

    def first_copies(self, k):
        pos = self.pos
        h0, h1 = self.halves
        copies = [
            self.copy(k, self.mine(k, pos.pd).at[h0], self.a0.at[k], self.s0, pos.xn),
            self.copy(k, self.mine(k, pos.px).at[h0], self.bx.at[k].at[h0], self.dx, pos.xn),
        ]
        if h1 is not None:
            copies += [
                self.copy(k, self.mine(k, pos.pd).at[h1], self.a1.at[k], self.s1, pos.yn),
                self.copy(k, self.mine(k, pos.py).at[h1], self.by.at[k].at[h1], self.dy, pos.yn),
            ]
        return copies

    def second_copies(self, k):
        pos = self.pos
        h0, h1 = self.halves
        copies = [
            self.copy(k, self.mine(k, pos.py).at[h0], self.by.at[k].at[h0], self.cy, pos.yn)
        ]
        if h1 is not None:
            copies.append(
                self.copy(k, self.mine(k, pos.px).at[h1], self.bx.at[k].at[h1], self.cx, pos.xn)
            )
        return copies

    def first(self, k):
        pos = self.pos
        z = pos.up(k)
        self.sibling_copy(k).wait_recv()
        for j in range(4):
            chip = pos.chip(3 - j)
            self.partial[z, chip, pos.c] = (
                self.partial[z, chip, pos.c].astype(F32) + self.theirs[z, chip].astype(F32)
            ).astype(self.partial.dtype)
        for copy in self.first_copies(k):
            copy.start()

    def landed(self, ref, sems, k):
        send(ref, ref, sems.at[0, k], sems.at[1, k], self.pos.xn).wait_recv()

    def second(self, k):
        pos = self.pos
        h0, h1 = self.halves
        copies = self.second_copies(k)
        self.landed(self.a0.at[k], self.s0, k)
        ref = self.mine(k, pos.py)
        ref[h0] = (ref[h0].astype(F32) + self.a0[k].astype(F32)).astype(ref.dtype)
        copies[0].start()
        if h1 is not None:
            self.landed(self.a1.at[k], self.s1, k)
            ref = self.mine(k, pos.px)
            ref[h1] = (ref[h1].astype(F32) + self.a1[k].astype(F32)).astype(ref.dtype)
            copies[1].start()

    def z_copy(self, k):
        pos = self.pos
        return send(
            self.bx.at[k], self.z.at[k], self.zs.at[0, k], self.zs.at[1, k], (pos.up(k), pos.s)
        )

    def third(self, k, total):
        pos = self.pos
        h0, h1 = self.halves
        self.landed(self.bx.at[k].at[h0], self.dx, k)
        self.landed(self.by.at[k].at[h0], self.cy, k)
        if h1 is not None:
            self.landed(self.by.at[k].at[h1], self.dy, k)
            self.landed(self.bx.at[k].at[h1], self.cx, k)
        total[...] = (
            self.mine(k, pos.p)[...].astype(F32)
            + self.bx[k].astype(F32)
            + self.by[k].astype(F32)
        )

        def on():
            self.bx[k] = total[...].astype(self.bx.dtype)
            self.z_copy(k).start()

        guarded(k != 0, on)

    def last(self, total):
        value = total[...]
        for k in range(1, self.pos.nb):
            self.landed(self.z.at[k], self.zs, k)
            value = value + self.z[k].astype(F32)
        total[...] = value

    def drain(self):
        def done(k, _):
            self.sibling_copy(k).wait_send()
            for copy in self.first_copies(k) + self.second_copies(k):
                copy.wait_send()
            guarded(k != 0, lambda: self.z_copy(k).wait_send())
            return 0

        lax.fori_loop(0, self.pos.nb, done, 0)


def half_shapes(shape, halves):
    def cut(half):
        return tuple(n if h == slice(None) else h.size for n, h in zip(shape, half))

    first = cut(halves[0])
    return first, (first if halves[1] is None else cut(halves[1]))


class RowScatter:
    def __init__(self, pos, out, bufs, sems):
        self.pos, self.out = pos, out
        self.mine, self.a0, self.a1, self.bx, self.by, self.far, self.near = bufs
        (self.sm,) = sems

    @staticmethod
    def scratch(rows, columns):
        return [
            pltpu.VMEM((rows, columns), BF16),
            pltpu.VMEM((rows, columns), BF16),
            pltpu.VMEM((2, rows, columns), BF16),
            pltpu.VMEM((2, rows, columns), BF16),
            pltpu.VMEM((rows, columns), F32),
            pltpu.VMEM((rows, columns), F32),
            DMA((2, 7)),
        ]

    def copy(self, i):
        pos, mine = self.pos, self.mine
        src, dst, there = (
            (mine.at[pos.pd, 0], self.a0, pos.xn),
            (mine.at[pos.pd, 1], self.a1, pos.yn),
            (mine.at[pos.px, 0], self.bx.at[0], pos.xn),
            (mine.at[pos.py, 1], self.by.at[1], pos.yn),
            (mine.at[pos.py, 0], self.by.at[0], pos.yn),
            (mine.at[pos.px, 1], self.bx.at[1], pos.xn),
            (self.far, self.near, pos.sib),
        )[i]
        return send(src, dst, self.sm.at[0, i], self.sm.at[1, i], there)

    def landed(self, i, ref):
        send(ref, ref, self.sm.at[0, i], self.sm.at[1, i], self.pos.xn).wait_recv()

    def first(self):
        for i in range(4):
            self.copy(i).start()

    def second(self):
        pos, mine = self.pos, self.mine
        self.landed(0, self.a0)
        mine[pos.py, 0] = (mine[pos.py, 0].astype(F32) + self.a0[...].astype(F32)).astype(BF16)
        self.copy(4).start()
        self.landed(1, self.a1)
        mine[pos.px, 1] = (mine[pos.px, 1].astype(F32) + self.a1[...].astype(F32)).astype(BF16)
        self.copy(5).start()

    def third(self):
        pos = self.pos
        self.landed(2, self.bx.at[0])
        self.landed(3, self.by.at[1])
        self.landed(4, self.by.at[0])
        self.landed(5, self.bx.at[1])

        def total(core):
            return (
                self.mine[pos.p, core].astype(F32)
                + self.bx[core].astype(F32)
                + self.by[core].astype(F32)
            )

        self.far[...] = total(1 - pos.c)
        self.copy(6).start()
        self.out[pos.c] += total(pos.c)

    def last(self):
        pos = self.pos
        self.landed(6, self.near)
        self.out[1 - pos.c] += self.near[...]
        for i in range(7):
            self.copy(i).wait_send()


class JointScatter:
    def __init__(self, pos, bufs, sems):
        self.pos = pos
        self.partial, self.theirs, self.zbuf, self.sums, self.got = bufs
        self.sb, self.zs, self.ps = sems

    @staticmethod
    def scratch(nb, shape):
        return [
            pltpu.VMEM((nb, 4, 2) + shape, BF16),
            pltpu.VMEM((nb, 4) + shape, BF16),
            pltpu.VMEM((nb, 4) + shape, BF16),
            pltpu.VMEM((4,) + shape, BF16),
            pltpu.VMEM((4,) + shape, BF16),
        ]

    @staticmethod
    def sem_scratch(nb):
        return [DMA((2,)), DMA((2, nb)), DMA((2, 4))]

    def sibling_copy(self):
        pos = self.pos
        return send(
            self.partial.at[:, :, 1 - pos.c], self.theirs, self.sb.at[0], self.sb.at[1], pos.sib
        )

    def z_copy(self, d):
        pos = self.pos
        return send(
            self.partial.at[pos.up(d), :, pos.c],
            self.zbuf.at[d],
            self.zs.at[0, d],
            self.zs.at[1, d],
            (pos.up(d), pos.s),
        )

    def plane_copy(self, k):
        pos = self.pos
        chip = pos.chip(k)
        return send(
            self.sums.at[chip],
            self.got.at[pos.p],
            self.ps.at[0, k],
            self.ps.at[1, k],
            (pos.b, 2 * chip + pos.c),
        )

    def begin(self):
        self.sibling_copy().start()

    def first(self):
        pos = self.pos
        self.sibling_copy().wait_recv()
        for d in (*range(1, pos.nb), 0):
            z = pos.up(d)
            self.partial[z, :, pos.c] = (
                self.partial[z, :, pos.c].astype(F32) + self.theirs[z].astype(F32)
            ).astype(BF16)
            if d:
                self.z_copy(d).start()

    def second(self):
        pos = self.pos
        value = self.partial[pos.b, :, pos.c].astype(F32)
        for d in range(1, pos.nb):
            self.z_copy(d).wait_recv()
            value = value + self.zbuf[d].astype(F32)
        self.sums[...] = value.astype(BF16)
        for k in range(1, 4):
            self.plane_copy(k).start()

    def last(self, out, vec):
        pos = self.pos
        width = out.shape[1] // 12
        self.got[pos.p] = self.sums[pos.p]
        for k in range(1, 4):
            ref = self.got.at[pos.chip(k)]
            send(ref, ref, self.ps.at[0, k], self.ps.at[1, k], pos.sib).wait_recv()
        extra = 0.0
        for chip in range(4):
            value = self.got[chip].astype(F32)
            for n in range(3):
                out[:, (4 * n + chip) * width : (4 * n + chip + 1) * width] = value[
                    :, n * width : (n + 1) * width
                ]
            extra = extra + value[:8, 3 * width : 3 * width + vec]
        self.sibling_copy().wait_send()
        for d in range(1, pos.nb):
            self.z_copy(d).wait_send()
        for k in range(1, 4):
            self.plane_copy(k).wait_send()
        return extra


def normed_rows(residual):
    centered = residual - jnp.mean(residual, axis=-1, keepdims=True)
    inverse = lax.rsqrt(jnp.mean(centered * centered, axis=-1, keepdims=True) + EPSILON)
    return centered * inverse, inverse


def transposed_dot(left, right):
    return lax.dot_general(left, right, (((0,), (0,)), ((), ())), preferred_element_type=F32)


def dot_transposed(left, right):
    return lax.dot_general(left, right, (((1,), (1,)), ((), ())), preferred_element_type=F32)


def feed_and_back(
    lengths, inputs, cotangent, mixed, vectors, hidden_bias,
    output_weight, expand_weight, reduce_weight, rows, weight, qkv, logs, nb, heads,
):
    _, count, model_width = inputs.shape
    hidden = hidden_bias.shape[1]
    block = hidden // nb
    width = heads * HEAD_DIM
    size, tokens = 8 * count, 2 * count
    owners = 8 * nb
    shard = vec = model_width // owners
    per = hidden // owners
    joint_shape = (shard, 3 * width + 64)
    shapes = [(16, 128), (shard, model_width), (shard, hidden), (per, model_width)]
    dtypes = [F32, BF16, BF16, BF16]

    def body(
        lengths_ref, inputs_ref, cotangent_ref, mixed_ref, vectors_ref, bias_ref,
        output_ref, expand_ref, reduce_ref, rows_any, weight_any, qkv_any, log_any,
        result_out, rows_out, joint_out, vectors_out, hidden_out,
        output_out, expand_out, reduce_out,
        output_w, expand_w, reduce_w, rows_ref, weight_ref, qkv_ref, log_ref, loads,
        context, first_normed, first_low, hidden_low, slope, feed, grad_low,
        grad_vectors, grad_bias, parts, small_total,
        grad_context, grad_qkv, grad_key, grad_value,
        *scratch,
    ):
        pos = Place(nb)
        scratch = list(scratch)

        def take(n):
            got = scratch[:n]
            del scratch[:n]
            return got

        mixing = ContextExchange(pos, parts, grad_context, take(2))
        row_sums = RowScatter(pos, rows_out, [hidden_low] + take(6), take(1))
        joints = JointScatter(pos, take(5), take(3))
        smalls, outputs, expands, reduces = (
            Scatter(pos, halves_of(shape), take(7), take(8)) for shape in shapes
        )

        def turn(i):
            return jnp.where(i < 2, 2 - i, 3 * (3 - i))

        def expand_load(z):
            at = pl.ds(z * block if isinstance(z, int) else pl.multiple_of(z * block, block), block)
            return pltpu.make_async_copy(expand_ref.at[:, at], expand_w.at[z], loads.at[z])

        def reduce_load(z):
            at = pl.ds(z * block if isinstance(z, int) else pl.multiple_of(z * block, block), block)
            return pltpu.make_async_copy(reduce_ref.at[at, :], reduce_w.at[z], loads.at[nb + z])

        output_load = pltpu.make_async_copy(output_ref, output_w, loads.at[2 * nb])
        later = [
            pltpu.make_async_copy(src, dst, loads.at[2 * nb + 1 + n])
            for n, (src, dst) in enumerate(
                ((rows_any, rows_ref), (weight_any, weight_ref), (qkv_any, qkv_ref), (log_any, log_ref))
            )
        ]
        output_load.start()
        for z in range(nb):
            expand_load(z).start()
            reduce_load(z).start()
        for copy in later:
            copy.start()
        barrier = pltpu.get_barrier_semaphore()
        partners = [(pos.up(d), pos.s) for d in range(1, nb)] + plane_others(pos)
        for device in partners:
            pl.semaphore_signal(barrier, inc=1, device_id=device, device_id_type=MESH)

        def vector(n):
            return vectors_ref[n : n + 1, :]

        for chip in range(4):
            context[:, chip * width : (chip + 1) * width] = mixed_ref[chip].reshape(tokens, width)
        output_load.wait()
        branch = jnp.dot(context[...], output_w[...], preferred_element_type=F32) + vector(4)
        normed, first_inverse = normed_rows(
            inputs_ref[...].reshape(tokens, model_width) + branch
        )
        first_normed[...] = normed
        first = normed * vector(0) + vector(1)
        rows_out[...] = first.reshape(2, count, model_width)
        first_low[...] = first.astype(BF16)
        feed[...] = jnp.broadcast_to(vector(7), feed.shape)

        def forward(z, _):
            at = pl.ds(pl.multiple_of(z * block, block), block)
            expand_load(z).wait()
            before = (
                jnp.dot(first_low[...], expand_w[z], preferred_element_type=F32)
                + bias_ref[:, at]
            )
            half = 0.5 * (1.0 + lax.erf(before * HALF_ROOT))
            low = (before * half).astype(BF16)
            hidden_low[z] = low.reshape(2, count, block)
            slope[z] = half + before * jnp.exp(-0.5 * before * before) * INV_ROOT_TAU
            reduce_load(z).wait()
            feed[...] += jnp.dot(low, reduce_w[z], preferred_element_type=F32)
            return 0

        lax.fori_loop(0, nb, forward, 0)
        normed, inverse = normed_rows(
            rows_out[...].reshape(tokens, model_width) + feed[...]
        )
        result_out[...] = (normed * vector(5) + vector(6)).reshape(2, count, model_width)

        places = pos.s * count + lax.broadcasted_iota(jnp.int32, (count, 1), 0)
        grad_res = jnp.concatenate(
            [jnp.where(places < lengths_ref[j], cotangent_ref[j], 0.0) for j in range(2)]
        )
        grad_second, gain, shift = norm_back(grad_res, normed, inverse, vector(5))
        grad_low[...] = grad_second.astype(BF16)
        grad_vectors[...] = jnp.zeros_like(grad_vectors)
        grad_vectors[5:6, :] = gain[None]
        grad_vectors[6:7, :] = shift[None]
        grad_vectors[7:8, :] = jnp.sum(grad_low[...].astype(F32), axis=0, keepdims=True)
        feed[...] = grad_second

        def backward(i, _):
            z = pos.up(turn(i))
            at = pl.ds(pl.multiple_of(z * block, block), block)
            for n in range(2):
                cut = slice(n * (block // 2), (n + 1) * (block // 2))
                reduces.partial[z, 2 * n : 2 * n + 2] = (
                    transposed_dot(
                        hidden_low[z, :, :, cut].reshape(tokens, block // 2), grad_low[...]
                    )
                    .reshape(2, 2, per, model_width)
                    .astype(BF16)
                )
            reduces.begin(turn(i))
            low = (dot_transposed(grad_low[...], reduce_w[z]) * slope[z]).astype(BF16)
            grad_bias[:, at] = jnp.sum(low.astype(F32), axis=0, keepdims=True)
            for n in range(2):
                cut = slice(n * (model_width // 2), (n + 1) * (model_width // 2))
                expands.partial[n * nb // 2 : (n + 1) * nb // 2, :, :, :, at] = (
                    transposed_dot(first_low[:, cut], low)
                    .reshape(nb // 2, 4, 2, shard, block)
                    .astype(BF16)
                )
            feed[...] += dot_transposed(low, expand_w[z])
            reduces.first(turn(i))
            return 0

        pl.semaphore_wait(barrier, len(partners))
        lax.fori_loop(0, nb, backward, 0)
        for k in range(nb):
            expands.begin(turn(k))
        grads, gain, shift = norm_back(feed[...], first_normed[...], first_inverse, vector(0))
        rows_out[...] = grads.reshape(2, count, model_width)
        low = grads.astype(BF16)
        grad_low[...] = low
        grad_vectors[0:1, :] = gain[None]
        grad_vectors[1:2, :] = shift[None]
        grad_vectors[4:5, :] = jnp.sum(low.astype(F32), axis=0, keepdims=True)
        low = dot_transposed(low, output_w[...]).astype(BF16)
        for chip in range(4):
            parts[chip] = low[:, chip * width : (chip + 1) * width].reshape(2, count, width)
        mixing.start()
        for n in range(2):
            cut = slice(n * (model_width // 2), (n + 1) * (model_width // 2))
            outputs.partial[n * nb // 2 : (n + 1) * nb // 2] = (
                transposed_dot(context[:, cut], grad_low[...])
                .reshape(nb // 2, 4, 2, shard, model_width)
                .astype(BF16)
            )
        for owner in range(owners):
            here = (owner // 8, owner % 8 // 2, owner % 2)
            smalls.partial[here] = jnp.concatenate(
                [
                    jnp.pad(
                        grad_vectors[:, owner * vec : (owner + 1) * vec], ((0, 0), (0, 128 - vec))
                    ),
                    jnp.broadcast_to(
                        jnp.pad(
                            grad_bias[:, owner * per : (owner + 1) * per], ((0, 0), (0, 128 - per))
                        ),
                        (8, 128),
                    ),
                ]
            )
        for k in range(nb):
            outputs.begin(turn(k))
            smalls.begin(turn(k))

        grad_key[...] = jnp.zeros_like(grad_key)
        grad_value[...] = jnp.zeros_like(grad_value)
        for copy in later:
            copy.wait()
        back = attend_back_block(
            lengths_ref[pos.c], qkv_ref, log_ref, grad_context, grad_qkv, grad_key, grad_value,
            heads, count,
        )

        def middle(i, _):
            k = turn(i)
            reduces.second(k)
            expands.first(k)
            guarded(i > 0, lambda: reduces.third(turn(i - 1), reduce_out))
            guarded(i == 0, mixing.arrive)
            back(i)
            return 0

        lax.fori_loop(0, nb, middle, 0)

        def late(i, _):
            k = turn(i)
            expands.second(k)
            outputs.first(k)
            smalls.first(k)
            return 0

        lax.fori_loop(0, 2, late, 0)
        grad_qkv[:, width : 2 * width] = (grad_key[...] * SCORE_SCALE).astype(BF16)
        grad_qkv[:, 2 * width :] = grad_value[...].astype(BF16)

        def spread(i, _):
            at = pl.ds(pl.multiple_of(i * tokens, tokens), tokens)
            row_sums.mine[i] = (
                dot_transposed(grad_qkv[at, :], weight_ref[...])
                .astype(BF16)
                .reshape(2, count, model_width)
            )
            return 0

        lax.fori_loop(0, 4, spread, 0)
        row_sums.first()
        for z in range(nb):
            grad_joint = transposed_dot(
                rows_ref[:, :, :, z * 8 * shard : (z + 1) * 8 * shard].reshape(size, 8 * shard),
                grad_qkv[...],
            )
            joints.partial[z, :, :, :, : 3 * width] = grad_joint.reshape(
                4, 2, shard, 3 * width
            ).astype(BF16)
        sums = jnp.sum(grad_qkv[...].astype(F32), axis=0, keepdims=True)
        joints.partial[:, :, :, :, 3 * width :] = jnp.zeros((nb, 4, 2, shard, 64), BF16)
        for s in range(8):
            at = slice(s * vec, (s + 1) * vec)
            value = jnp.concatenate([sums[:, :width][:, at], sums[:, 2 * width :][:, at]])
            joints.partial[pos.p, s // 2, s % 2, :, 3 * width :] = jnp.pad(
                value, ((0, shard - 2), (0, 64 - vec))
            ).astype(BF16)
        joints.begin()
        lax.fori_loop(2, nb, late, 0)
        joints.first()

        def summed(i, _):
            expands.third(turn(i), expand_out)
            return 0

        lax.fori_loop(0, nb - 1, summed, 0)
        reduces.third(turn(nb - 1), reduce_out)
        reduces.last(reduce_out)
        reduces.drain()
        row_sums.second()

        def final(i, _):
            k = turn(i)
            outputs.second(k)
            smalls.second(k)
            return 0

        lax.fori_loop(0, nb, final, 0)
        expands.third(turn(nb - 1), expand_out)
        joints.second()
        row_sums.third()
        expands.last(expand_out)
        expands.drain()
        mixing.drain()

        def end(i, _):
            k = turn(i)
            outputs.third(k, output_out)
            smalls.third(k, small_total)
            return 0

        lax.fori_loop(0, nb, end, 0)
        extra = joints.last(joint_out, vec)
        row_sums.last()
        for scatter, out in ((outputs, output_out), (smalls, small_total)):
            scatter.last(out)
            scatter.drain()
        lines = lax.broadcasted_iota(jnp.int32, (8, vec), 0)
        value = jnp.where(lines == 2, extra[0:1], small_total[:8, :vec])
        vectors_out[...] = jnp.where(lines == 3, extra[1:2], value)
        hidden_out[...] = small_total[8:9, :per]

    def vmem(shape, dtype):
        return pltpu.VMEM(shape, dtype)

    scratch = [
        vmem((model_width, model_width), BF16),
        vmem((nb, model_width, block), BF16),
        vmem((nb, block, model_width), BF16),
        vmem(rows.shape, BF16),
        vmem(weight.shape, BF16),
        vmem(qkv.shape, BF16),
        vmem(logs.shape, F32),
        DMA((2 * nb + 5,)),
        vmem((tokens, model_width), BF16),
        vmem((tokens, model_width), F32),
        vmem((tokens, model_width), BF16),
        vmem((nb, 2, count, block), BF16),
        vmem((nb, tokens, block), F32),
        vmem((tokens, model_width), F32),
        vmem((tokens, model_width), BF16),
        vmem((8, model_width), F32),
        vmem((1, hidden), F32),
        vmem((4, 2, count, width), BF16),
        vmem((16, 128), F32),
        vmem((4, 2, count, width), BF16),
        vmem((size, 3 * width), BF16),
        vmem((size, width), F32),
        vmem((size, width), F32),
    ]
    scratch += ContextExchange.scratch() + RowScatter.scratch(count, model_width)
    scratch += JointScatter.scratch(nb, joint_shape) + JointScatter.sem_scratch(nb)
    for shape, dtype in zip(shapes, dtypes):
        scratch += Scatter.scratch(nb, shape, dtype, halves_of(shape)) + Scatter.sem_scratch(nb)
    return pl.pallas_call(
        body,
        out_shape=tuple(
            jax.ShapeDtypeStruct(shape, F32)
            for shape in (
                inputs.shape,
                inputs.shape,
                (shard, 3 * model_width),
                (8, vec),
                (1, per),
                shapes[1],
                shapes[2],
                shapes[3],
            )
        ),
        in_specs=[SM] + [VM] * 5 + [ANY] * 7,
        out_specs=(VM,) * 8,
        scratch_shapes=scratch,
        name="feed_and_back",
        compiler_params=pltpu.CompilerParams(
            collective_id=4, has_side_effects=True, vmem_limit_bytes=VMEM_LIMIT
        ),
    )(
        lengths, inputs, cotangent, mixed, vectors, hidden_bias,
        output_weight, expand_weight, reduce_weight, rows, weight, qkv, logs,
    )


def hand_over(*arrays):
    count = len(arrays)

    def body(*refs):
        came, out, held = refs[:count], refs[count : 2 * count], refs[2 * count : 3 * count]
        sems = refs[3 * count]
        loads = [pltpu.make_async_copy(came[n], held[n], sems.at[0, n]) for n in range(count)]
        stores = [pltpu.make_async_copy(held[n], out[n], sems.at[1, n]) for n in range(count)]
        for copy in loads:
            copy.start()
        for load, store in zip(loads, stores):
            load.wait()
            store.start()
        for copy in stores:
            copy.wait()

    return pl.pallas_call(
        body,
        out_shape=tuple(jax.ShapeDtypeStruct(a.shape, a.dtype) for a in arrays),
        in_specs=[ANY] * count,
        out_specs=(ANY,) * count,
        scratch_shapes=[pltpu.VMEM(a.shape, a.dtype) for a in arrays] + [DMA((2, count))],
        name="hand_over",
        compiler_params=pltpu.CompilerParams(vmem_limit_bytes=VMEM_LIMIT),
    )(*arrays)


def plane_on_device(
    inputs,
    cotangent,
    lengths,
    joint_weight,
    output_weight,
    vectors,
    expand_weight,
    expand_bias,
    reduce_weight,
):
    nb = lax.axis_size("batch")
    _, _, model_width = inputs.shape
    hidden_width = expand_weight.shape[1]
    heads = model_width // (4 * HEAD_DIM)
    per = expand_bias.shape[0]
    (
        vector_rows, full_bias, rows_all, joint_all, qkv, logs,
        mixed, output_all, expand_all, reduce_all,
    ) = gather_attend(
        lengths,
        inputs,
        joint_weight,
        vectors,
        expand_bias.reshape(1, per),
        output_weight,
        expand_weight,
        reduce_weight,
        nb,
        heads,
    )
    full_output = output_all.reshape(model_width, model_width)
    full_expand = expand_all.reshape(model_width, hidden_width)
    full_reduce = reduce_all.reshape(hidden_width, model_width)

    result, grad_inputs, joint_sum, vectors_sum, bias_sum, output_sum, expand_sum, reduce_sum = (
        feed_and_back(
            lengths,
            inputs,
            cotangent,
            mixed,
            vector_rows,
            full_bias,
            full_output,
            full_expand,
            full_reduce,
            rows_all,
            joint_all,
            qkv,
            logs,
            nb,
            heads,
        )
    )
    (
        result, grad_inputs, joint_sum, output_sum, vectors_sum, expand_sum, bias_sum, reduce_sum,
    ) = hand_over(
        result, grad_inputs, joint_sum, output_sum, vectors_sum, expand_sum, bias_sum, reduce_sum
    )
    return (
        result,
        grad_inputs,
        joint_sum,
        output_sum,
        vectors_sum,
        expand_sum,
        bias_sum.reshape(per),
        reduce_sum,
    )


def plane_fits(mesh, inputs, expand_bias, expand_weight):
    return (
        mesh.shape["seq"] == 8
        and mesh.shape["batch"] == 4
        and inputs[0] == 2 * mesh.shape["batch"]
        and HEADS % 4 == 0
        and inputs[2] == HEADS * HEAD_DIM
        and inputs[1] % (8 * 16) == 0
        and inputs[2] % 256 == 0
        and expand_weight[0] % (8 * 32) == 0
        and expand_weight[1] % (16 * 32) == 0
        and expand_bias[0] <= 128 * 32
        and expand_weight[1] == 4 * inputs[2]
    )


def solution(mesh):
    def program(*args):
        fits = plane_fits(mesh, args[0].shape, args[7].shape, args[6].shape)
        return jax.shard_map(
            plane_on_device if fits else general_on_device,
            mesh=mesh,
            in_specs=(
                P("batch", "seq", None),
                P("batch", "seq", None),
                P("batch"),
                P(("batch", "seq"), None),
                P(("batch", "seq"), None),
                P(None, ("batch", "seq")),
                P(("batch", "seq"), None),
                P(("batch", "seq")),
                P(("batch", "seq"), None),
            ),
            out_specs=(
                P("batch", "seq", None),
                P("batch", "seq", None),
                P(("batch", "seq"), None),
                P(("batch", "seq"), None),
                P(None, ("batch", "seq")),
                P(("batch", "seq"), None),
                P(("batch", "seq")),
                P(("batch", "seq"), None),
            ),
            check_vma=False,
        )(*args)

    return program
```

profile of v0, /device:TPU:0, one launch (start us, length us, event | category | flops | bytes accessed | tf_op | source)
XLA Modules:
  0.0 163.6 jit_solution(14034940085083988116)
XLA Ops:
  0.6 72.9 %gather_attend.1 = (f32[8,768]{1,0:T(8,128)}, f32[1,3072]{1,0:T(1,128)}, bf16[4,2,128,768]{3,2,1,0:T(8,128)(2,1)}, bf16[768,576]{1,0:T(8,128)(2,1)}, bf16[1024,5...) custom-call(s32[2]{0:T(128)} %lengths_ref.3, ...), custom_call_target="tpu_custom_call" | custom-call | tf_op jit(solution)/shard_map/gather_attend/pallas_call | solution.py:920
  73.6 87.2 %feed_and_back.1 = (f32[2,128,768]{2,1,0:T(8,128)}, f32[2,128,768]{2,1,0:T(8,128)}, f32[24,2304]{1,0:T(8,128)}, f32[8,24]{1,0:T(8,128)}, f32[1,96]{1,0:T(1,128)}...) custom-call(s32[2]{0:T(128)} %lengths_ref.3, f32[2,128,768]{2,1,0:T(8,128)} %inputs_ref.3, ...), custom_call_target="tpu_custom_call" | custom-call | tf_op jit(solution)/shard_map/feed_and_back/pallas_call | solution.py:1711
  160.8 2.7 %hand_over.1 = (f32[2,128,768]{2,1,0:T(8,128)}, f32[2,128,768]{2,1,0:T(8,128)}, f32[24,2304]{1,0:T(8,128)}, f32[24,768]{1,0:T(8,128)}, f32[8,24]{1,0:T(8,128)}, ...) custom-call(f32[2,128,768]{2,1,0:T(8,128)} %get-tuple-element.44.refs_0_, ...), custom_call_target="tpu_custom_call" | custom-call | tf_op jit(solution)/shard_map/hand_over/pallas_call | solution.py:1755
where the time goes:
time: 164 us
  Pallas kernels  163 us (99%)
    pallas_call x1, Pallas kernels, feed_and_back(): pl.pallas_call(body, out_shape=tuple((jax.ShapeDtypeStruct(shape, F32) fo...  87.2 us
    pallas_call x1, Pallas kernels, gather_attend(): pl.pallas_call(body, out_shape=(jax.ShapeDtypeStruct((8, model_width), F3...  72.9 us

commit v1 on v0

--- a/solution.py
+++ b/solution.py
@@ -451,8 +451,7 @@
 
 
 class Gather:
-    def __init__(self, pos, shard, out, halves, tall, sems):
-        self.tall = tall
+    def __init__(self, pos, shard, out, halves, sems):
         self.pos, self.shard, self.out, self.halves = pos, shard, out, halves
         self.xs, self.ys, self.f0, self.f1, self.sb, self.local_sem = sems[:6]
         self.chain = Chain(pos, shard, lambda z: out.at[z, pos.p, pos.c], sems[6:8])
@@ -462,7 +461,7 @@
 
     @staticmethod
     def scratch(nb):
-        return [DMA((2, nb))] * 5 + [DMA] + Chain.scratch(nb) * 2
+        return [DMA((2, nb))] * 2 + [DMA((2,))] * 2 + [DMA((2, nb + 3)), DMA] + Chain.scratch(nb) * 2
 
     def z(self, k):
         return jnp.where(k <= self.pos.b, self.pos.b - k, k)
@@ -495,67 +494,72 @@
         ref = self.out.at[self.z(k), chip, pos.c]
         send(ref, ref, sems.at[0, k], sems.at[1, k], pos.xn).wait_recv()
 
-    def y_forward(self, k):
-        pos = self.pos
-        ref = self.out.at[self.z(k), pos.px, pos.c].at[self.halves[0]]
-        return send(ref, ref, self.f0.at[0, k], self.f0.at[1, k], pos.yn)
-
-    def x_forward(self, k):
-        pos = self.pos
-        ref = self.out.at[self.z(k), pos.py, pos.c].at[self.halves[1]]
-        return send(ref, ref, self.f1.at[0, k], self.f1.at[1, k], pos.xn)
-
-    def two_ways(self, k):
-        return True if not self.tall else k == 0
-
-    def forward(self, k):
-        pos = self.pos
-        self.landed(self.xs, k, pos.px)
-        guarded(self.two_ways(k), lambda: self.y_forward(k).start())
-        self.landed(self.ys, k, pos.py)
+    def y_forward(self):
+        pos = self.pos
+        ref = self.out.at[pos.b, pos.px, pos.c].at[self.halves[0]]
+        return send(ref, ref, self.f0.at[0], self.f0.at[1], pos.yn)
+
+    def x_forward(self):
+        pos = self.pos
+        ref = self.out.at[pos.b, pos.py, pos.c].at[self.halves[1]]
+        return send(ref, ref, self.f1.at[0], self.f1.at[1], pos.xn)
+
+    def forward(self):
+        pos = self.pos
+        self.landed(self.xs, 0, pos.px)
+        self.y_forward().start()
+        self.landed(self.ys, 0, pos.py)
         if self.halves[1] is not None:
-            guarded(self.two_ways(k), lambda: self.x_forward(k).start())
-
-    def crossed(self, k):
-        pos = self.pos
-        across = self.out.at[self.z(k), pos.pd, pos.c]
+            self.x_forward().start()
+
+    def cross(self):
+        pos = self.pos
+        across = self.out.at[pos.b, pos.pd, pos.c]
         for half, sems in zip(self.halves, (self.f0, self.f1)):
             if half is not None:
                 ref = across.at[half]
-                send(ref, ref, sems.at[0, k], sems.at[1, k], pos.xn).wait_recv()
-
-    def complete(self, k):
-        if not self.tall:
-            self.crossed(k)
-        elif isinstance(k, int) and k == 0:
-            self.crossed(k)
-            self.across.start()
-        else:
-            self.across.hop(k)
-
-    def sibling_copy(self, k):
-        pos = self.pos
-        ref = self.out.at[self.z(k), :, pos.c]
+                send(ref, ref, sems.at[0], sems.at[1], pos.xn).wait_recv()
+
+    def beside(self, k):
+        pos = self.pos
+        self.landed(self.xs, k, pos.px)
+        self.landed(self.ys, k, pos.py)
+
+    def sibling_copy(self, k, core=None):
+        pos = self.pos
+        ref = self.out.at[self.z(k), :, pos.c if core is None else core]
         return send(ref, ref, self.sb.at[0, k], self.sb.at[1, k], pos.sib)
 
     def sibling(self, k):
         self.sibling_copy(k).start()
 
+    def part_copy(self, n, core=None):
+        pos = self.pos
+        k = pos.nb - 1
+        ref = self.out.at[self.z(k), pos.chip(n), pos.c if core is None else core]
+        return send(ref, ref, self.sb.at[0, k + n], self.sb.at[1, k + n], pos.sib)
+
     def finish(self, k):
-        pos = self.pos
-        ref = self.out.at[self.z(k), :, 1 - pos.c]
-        send(ref, ref, self.sb.at[0, k], self.sb.at[1, k], pos.sib).wait_recv()
+        self.sibling_copy(k, 1 - self.pos.c).wait_recv()
         self.x_copy(k).wait_send()
         self.y_copy(k).wait_send()
         self.sibling_copy(k).wait_send()
-        guarded(self.two_ways(k), lambda: self.y_forward(k).wait_send())
+
+    def end(self):
+        k = self.pos.nb - 1
+        for n in range(4):
+            self.part_copy(n, 1 - self.pos.c).wait_recv()
+        for n in range(4):
+            self.part_copy(n).wait_send()
+        self.x_copy(k).wait_send()
+        self.y_copy(k).wait_send()
+
+    def drain(self):
+        self.y_forward().wait_send()
         if self.halves[1] is not None:
-            guarded(self.two_ways(k), lambda: self.x_forward(k).wait_send())
-
-    def drain(self):
+            self.x_forward().wait_send()
         self.chain.drain()
-        if self.tall:
-            self.across.drain()
+        self.across.drain()
 
 
 class InputExchange:
@@ -757,12 +761,12 @@
         joints = JointGather(pos, joint_ref, joint_all, take(5))
         mixing = ContextExchange(pos, context, context_out, take(2))
         outputs, expands, reduces, smalls = (
-            Gather(pos, part, out, halves_of(part.shape), tall, take(10))
-            for part, out, tall in (
-                (output_ref, output_out, True),
-                (expand_ref, expand_out, True),
-                (reduce_ref, reduce_out, True),
-                (small_ref, small_all, True),
+            Gather(pos, part, out, halves_of(part.shape), take(10))
+            for part, out in (
+                (output_ref, output_out),
+                (expand_ref, expand_out),
+                (reduce_ref, reduce_out),
+                (small_ref, small_all),
             )
         )
         gathers = (expands, smalls, reduces, outputs)
@@ -811,12 +815,13 @@
             for gather in gathers:
                 gather.chain.hop(k)
 
-        def hand_on(k, some):
+        def relay(k, some):
             for gather in some:
-                gather.complete(k)
-            for gather in some:
-                if k:
-                    gather.forward(k)
+                gather.across.hop(k)
+
+        def share(k):
+            for gather in gathers:
+                gather.beside(k)
                 gather.sibling(k)
 
         attend = attend_block(lengths_ref[pos.c], qkv_out, log_out, context, heads, count)
@@ -849,61 +854,68 @@
             gather.plane(0, gather.shard)
         joints.own()
         for n, gather in enumerate(gathers):
-            gather.local.wait()
-            gather.forward(0)
+            gather.forward()
             if n == 1:
                 exchange.start()
         hop(1)
         joints.chain.hop(1)
-        hand_on(0, gathers)
-        spread(1)
+        for gather in gathers:
+            gather.local.wait()
+            gather.cross()
+            gather.sibling(0)
         joints.chain.hop(2)
         hop(2)
+        for gather in gathers:
+            gather.across.start()
         exchange.forward()
+        spread(1)
         joints.chain.hop(3)
         joints.sibling()
+        exchange.finish()
+        spread(2)
+        prepare()
         hop(3)
-        for gather in units[0]:
-            gather.plane(2)
-        exchange.finish()
-        for unit in units[1:]:
-            for gather in unit:
-                gather.plane(2)
         spread(3)
-        prepare()
-        hand_on(1, gathers)
-        for i in range(3):
-            attend(i)
-        hand_on(2, gathers)
+        attend(0)
+        relay(1, gathers)
+        attend(1)
+        attend(2)
+        relay(2, gathers)
         attend(3)
         mixing.start()
         saves[3].start()
-        hand_on(nb - 1, (smalls,))
-
-        def finish(some):
-            def done(k, _):
-                for gather in some:
-                    gather.finish(k)
-                return 0
-
-            return done
-
-        lax.fori_loop(0, nb, finish((smalls,)), 0)
+        share(1)
+        relay(nb - 1, (smalls,))
+        share(2)
+        for gather in gathers:
+            gather.beside(nb - 1)
+            for n in range(3):
+                gather.part_copy(n).start()
+        smalls.part_copy(3).start()
+
+        def finish(k, _):
+            for gather in gathers:
+                gather.finish(k)
+            return 0
+
+        lax.fori_loop(0, nb - 1, finish, 0)
+        smalls.end()
         for owner in range(8 * nb):
             part = small_all[owner // 8, owner % 8 // 2, owner % 2].astype(F32)
             vectors_out[:, owner * vec : (owner + 1) * vec] = part[:8, :vec]
             hidden_out[:, owner * per : (owner + 1) * per] = part[8:9, :per]
-        large = (expands, reduces, outputs)
-        lax.fori_loop(0, nb - 1, finish(large), 0)
         smalls.drain()
-        mixing.arrive()
         exchange.drain()
         joints.drain()
+        for gather in (expands, reduces, outputs):
+            gather.across.hop(nb - 1)
+            gather.part_copy(3).start()
+        for gather in (expands, reduces, outputs):
+            gather.drain()
+        mixing.arrive()
         mixing.drain()
-        hand_on(nb - 1, large)
-        for gather in large:
-            gather.drain()
-        finish(large)(nb - 1, 0)
+        for gather in (expands, reduces, outputs):
+            gather.end()
         for copy in saves:
             copy.wait()
 

time: 164 us -> 160 us (0.976)
  Pallas kernels: 163 us -> 159 us
    pallas_call x1, Pallas kernels: 72.9 us -> 68.4 us  [gather_attend(): pl.pallas_call(body, out_shape=(jax.ShapeDtypeStruct((8, model_width), F3...]
where the time goes in v1:
time: 160 us; the launch traced here: 159 us
  Pallas kernels  159 us (99%)
    pallas_call x1, Pallas kernels, feed_and_back(): pl.pallas_call(body, out_shape=tuple((jax.ShapeDtypeStruct(shape, F32) fo...  87.5 us
    pallas_call x1, Pallas kernels, gather_attend(): pl.pallas_call(body, out_shape=(jax.ShapeDtypeStruct((8, model_width), F3...  68.4 us

profile of v1, /device:TPU:0, one launch (start us, length us, event | category | flops | bytes accessed | tf_op | source)
XLA Modules:
  0.0 159.5 jit_solution(188134543551453890)
XLA Ops:
  0.6 68.4 %gather_attend.1 = (f32[8,768]{1,0:T(8,128)}, f32[1,3072]{1,0:T(1,128)}, bf16[4,2,128,768]{3,2,1,0:T(8,128)(2,1)}, bf16[768,576]{1,0:T(8,128)(2,1)}, bf16[1024,5...) custom-call(s32[2]{0:T(128)} %lengths_ref.3, ...), custom_call_target="tpu_custom_call" | custom-call | tf_op jit(solution)/shard_map/gather_attend/pallas_call | solution.py:932
  69.1 87.5 %feed_and_back.1 = (f32[2,128,768]{2,1,0:T(8,128)}, f32[2,128,768]{2,1,0:T(8,128)}, f32[24,2304]{1,0:T(8,128)}, f32[8,24]{1,0:T(8,128)}, f32[1,96]{1,0:T(1,128)}...) custom-call(s32[2]{0:T(128)} %lengths_ref.3, f32[2,128,768]{2,1,0:T(8,128)} %inputs_ref.3, ...), custom_call_target="tpu_custom_call" | custom-call | tf_op jit(solution)/shard_map/feed_and_back/pallas_call | solution.py:1723
  156.6 2.7 %hand_over.1 = (f32[2,128,768]{2,1,0:T(8,128)}, f32[2,128,768]{2,1,0:T(8,128)}, f32[24,2304]{1,0:T(8,128)}, f32[24,768]{1,0:T(8,128)}, f32[8,24]{1,0:T(8,128)}, ...) custom-call(f32[2,128,768]{2,1,0:T(8,128)} %get-tuple-element.44.refs_0_, ...), custom_call_target="tpu_custom_call" | custom-call | tf_op jit(solution)/shard_map/hand_over/pallas_call | solution.py:1767

commit v2 on v1

--- a/solution.py
+++ b/solution.py
@@ -367,8 +367,11 @@
     last = pos.nb - 1
     guarded(pos.b < last, lambda: signal(((pos.b + 1) % pos.nb, pos.s)))
     guarded(pos.b > 0, lambda: signal(((pos.b + last) % pos.nb, pos.s)))
-    beside = jnp.where(pos.b < last, 1, 0) + jnp.where(pos.b > 0, 1, 0)
-    pl.semaphore_wait(barrier, 7 + beside)
+
+
+def meet_near(pos):
+    beside = jnp.where(pos.b < pos.nb - 1, 1, 0) + jnp.where(pos.b > 0, 1, 0)
+    pl.semaphore_wait(pltpu.get_barrier_semaphore(), 7 + beside)
 
 
 def same_core(pos):
@@ -830,6 +833,7 @@
             for gather in gathers:
                 gather.plane(k)
 
+        greet_near(pos)
         weight = joint_weight_ref[...]
         spot = jnp.pad(
             own_vectors_ref[2:4, :].astype(F32), ((0, shard - 2), (0, 64 - vec))
@@ -845,13 +849,13 @@
                 jnp.pad(own_bias_ref[...].astype(F32), ((0, 7), (0, 128 - per))),
             ]
         ).astype(BF16)
-        rows_ref[...] = inputs_ref[...].astype(BF16)
-        greet_near(pos)
+        meet_near(pos)
         joints.start()
         for gather in gathers:
             gather.own()
             gather.chain.start()
             gather.plane(0, gather.shard)
+        rows_ref[...] = inputs_ref[...].astype(BF16)
         joints.own()
         for n, gather in enumerate(gathers):
             gather.forward()
@@ -935,7 +939,7 @@
             jax.ShapeDtypeStruct((8, model_width), F32),
             jax.ShapeDtypeStruct((1, 8 * nb * per), F32),
             *(jax.ShapeDtypeStruct(shape, dtype) for shape, dtype in kept),
-            jax.ShapeDtypeStruct((4, 2, count, width), BF16),
+            jax.ShapeDtypeStruct((4, 2, count // 2, 2 * width), BF16),
             shape(output),
             shape(expand),
             shape(reduce),
@@ -946,7 +950,7 @@
         + [DMA((4,))]
         + [
             pltpu.VMEM((nb, 4, 2) + joint_shape[1:], BF16),
-            pltpu.VMEM((4, 2, count, width), BF16),
+            pltpu.VMEM((4, 2, count // 2, 2 * width), BF16),
             pltpu.VMEM((nb, 4, 2) + small_shape, BF16),
             pltpu.VMEM((1, 3 * width), F32),
             pltpu.VMEM(inputs.shape, BF16),
@@ -1010,7 +1014,7 @@
             mixed = jnp.dot(exps.astype(BF16), value, preferred_element_type=F32)
             parts.append(mixed / total)
             logs = jnp.where(lanes == h, top + jnp.log(total), logs)
-        context_ref[n // 2, n % 2] = jnp.concatenate(parts, axis=1).astype(BF16)
+        context_ref[n // 2, n % 2] = packed(jnp.concatenate(parts, axis=1)).astype(BF16)
         log_ref[at, :] = logs
         return 0
 
@@ -1018,6 +1022,16 @@
         lax.fori_loop(2 * i, 2 * i + 2, part, 0)
 
     return block
+
+
+def packed(rows):
+    half = rows.shape[0] // 2
+    return jnp.concatenate([rows[:half], rows[half:]], axis=1)
+
+
+def unpacked(rows):
+    half = rows.shape[1] // 2
+    return jnp.concatenate([rows[:, :half], rows[:, half:]], axis=0)
 
 
 def attend_back_block(limit, qkv_ref, log_ref, grad_ref, grad_qkv, grad_key, grad_value, heads, count):
@@ -1029,7 +1043,7 @@
     def part(n, _):
         at = pl.ds(pl.multiple_of(n * count, count), count)
         allowed = lax.broadcasted_iota(jnp.int32, (1, size), 1) < limit
-        grads = grad_ref[n // 2, n % 2]
+        grads = unpacked(grad_ref[n // 2, n % 2])
         parts = []
         for h in range(heads):
             query = qkv_ref[at, h * HEAD_DIM : (h + 1) * HEAD_DIM]
@@ -1083,7 +1097,7 @@
             pltpu.VMEM((nb,) + second, dtype),
             pltpu.VMEM((nb,) + shape, dtype),
             pltpu.VMEM((nb,) + shape, dtype),
-            pltpu.VMEM((nb,) + shape, dtype),
+            pltpu.VMEM((nb - 1,) + shape, dtype),
         ]
 
     @staticmethod
@@ -1168,7 +1182,7 @@
     def z_copy(self, k):
         pos = self.pos
         return send(
-            self.bx.at[k], self.z.at[k], self.zs.at[0, k], self.zs.at[1, k], (pos.up(k), pos.s)
+            self.bx.at[k], self.z.at[k - 1], self.zs.at[0, k], self.zs.at[1, k], (pos.up(k), pos.s)
         )
 
     def third(self, k, total):
@@ -1194,8 +1208,8 @@
     def last(self, total):
         value = total[...]
         for k in range(1, self.pos.nb):
-            self.landed(self.z.at[k], self.zs, k)
-            value = value + self.z[k].astype(F32)
+            self.landed(self.z.at[k - 1], self.zs, k)
+            value = value + self.z[k - 1].astype(F32)
         total[...] = value
 
     def drain(self):
@@ -1301,7 +1315,7 @@
         return [
             pltpu.VMEM((nb, 4, 2) + shape, BF16),
             pltpu.VMEM((nb, 4) + shape, BF16),
-            pltpu.VMEM((nb, 4) + shape, BF16),
+            pltpu.VMEM((nb - 1, 4) + shape, BF16),
             pltpu.VMEM((4,) + shape, BF16),
             pltpu.VMEM((4,) + shape, BF16),
         ]
@@ -1320,7 +1334,7 @@
         pos = self.pos
         return send(
             self.partial.at[pos.up(d), :, pos.c],
-            self.zbuf.at[d],
+            self.zbuf.at[d - 1],
             self.zs.at[0, d],
             self.zs.at[1, d],
             (pos.up(d), pos.s),
@@ -1356,7 +1370,7 @@
         value = self.partial[pos.b, :, pos.c].astype(F32)
         for d in range(1, pos.nb):
             self.z_copy(d).wait_recv()
-            value = value + self.zbuf[d].astype(F32)
+            value = value + self.zbuf[d - 1].astype(F32)
         self.sums[...] = value.astype(BF16)
         for k in range(1, 4):
             self.plane_copy(k).start()
@@ -1473,7 +1487,10 @@
             return vectors_ref[n : n + 1, :]
 
         for chip in range(4):
-            context[:, chip * width : (chip + 1) * width] = mixed_ref[chip].reshape(tokens, width)
+            for j in range(2):
+                context[j * count : (j + 1) * count, chip * width : (chip + 1) * width] = unpacked(
+                    mixed_ref[chip, j]
+                )
         output_load.wait()
         branch = jnp.dot(context[...], output_w[...], preferred_element_type=F32) + vector(4)
         normed, first_inverse = normed_rows(
@@ -1557,7 +1574,10 @@
         grad_vectors[4:5, :] = jnp.sum(low.astype(F32), axis=0, keepdims=True)
         low = dot_transposed(low, output_w[...]).astype(BF16)
         for chip in range(4):
-            parts[chip] = low[:, chip * width : (chip + 1) * width].reshape(2, count, width)
+            for j in range(2):
+                parts[chip, j] = packed(
+                    low[j * count : (j + 1) * count, chip * width : (chip + 1) * width]
+                )
         mixing.start()
         for n in range(2):
             cut = slice(n * (model_width // 2), (n + 1) * (model_width // 2))
@@ -1601,18 +1621,18 @@
             guarded(i > 0, lambda: reduces.third(turn(i - 1), reduce_out))
             guarded(i == 0, mixing.arrive)
             back(i)
+            guarded(i > 0, lambda: expands.second(turn(i - 1)))
+            guarded(i > 1, lambda: expands.third(turn(i - 2), expand_out))
             return 0
 
         lax.fori_loop(0, nb, middle, 0)
 
         def late(i, _):
             k = turn(i)
-            expands.second(k)
             outputs.first(k)
             smalls.first(k)
             return 0
 
-        lax.fori_loop(0, 2, late, 0)
         grad_qkv[:, width : 2 * width] = (grad_key[...] * SCORE_SCALE).astype(BF16)
         grad_qkv[:, 2 * width :] = grad_value[...].astype(BF16)
 
@@ -1625,8 +1645,6 @@
             )
             return 0
 
-        lax.fori_loop(0, 4, spread, 0)
-        row_sums.first()
         for z in range(nb):
             grad_joint = transposed_dot(
                 rows_ref[:, :, :, z * 8 * shard : (z + 1) * 8 * shard].reshape(size, 8 * shard),
@@ -1644,14 +1662,13 @@
                 value, ((0, shard - 2), (0, 64 - vec))
             ).astype(BF16)
         joints.begin()
-        lax.fori_loop(2, nb, late, 0)
+        lax.fori_loop(0, 4, spread, 0)
+        row_sums.first()
         joints.first()
-
-        def summed(i, _):
-            expands.third(turn(i), expand_out)
-            return 0
-
-        lax.fori_loop(0, nb - 1, summed, 0)
+        expands.second(turn(3))
+        lax.fori_loop(0, nb, late, 0)
+
+        expands.third(turn(2), expand_out)
         reduces.third(turn(nb - 1), reduce_out)
         reduces.last(reduce_out)
         reduces.drain()
@@ -1709,9 +1726,9 @@
         vmem((tokens, model_width), BF16),
         vmem((8, model_width), F32),
         vmem((1, hidden), F32),
-        vmem((4, 2, count, width), BF16),
+        vmem((4, 2, count // 2, 2 * width), BF16),
         vmem((16, 128), F32),
-        vmem((4, 2, count, width), BF16),
+        vmem((4, 2, count // 2, 2 * width), BF16),
         vmem((size, 3 * width), BF16),
         vmem((size, width), F32),
         vmem((size, width), F32),

time: 160 us -> 158 us (0.988)
  Pallas kernels: 159 us -> 157 us
where the time goes in v2:
time: 158 us
  Pallas kernels  157 us (99%)
    pallas_call x1, Pallas kernels, feed_and_back(): pl.pallas_call(body, out_shape=tuple((jax.ShapeDtypeStruct(shape, F32) fo...  86.1 us
    pallas_call x1, Pallas kernels, gather_attend(): pl.pallas_call(body, out_shape=(jax.ShapeDtypeStruct((8, model_width), F3...  68.5 us

profile of v2, /device:TPU:0, one launch (start us, length us, event | category | flops | bytes accessed | tf_op | source)
XLA Modules:
  0.0 158.1 jit_solution(12418361208707401162)
XLA Ops:
  0.6 68.5 %gather_attend.1 = (f32[8,768]{1,0:T(8,128)}, f32[1,3072]{1,0:T(1,128)}, bf16[4,2,128,768]{3,2,1,0:T(8,128)(2,1)}, bf16[768,576]{1,0:T(8,128)(2,1)}, bf16[1024,5...) custom-call(s32[2]{0:T(128)} %lengths_ref.3, ...), custom_call_target="tpu_custom_call" | custom-call | tf_op jit(solution)/shard_map/gather_attend/pallas_call | solution.py:936
  69.1 86.1 %feed_and_back.1 = (f32[2,128,768]{2,1,0:T(8,128)}, f32[2,128,768]{2,1,0:T(8,128)}, f32[24,2304]{1,0:T(8,128)}, f32[8,24]{1,0:T(8,128)}, f32[1,96]{1,0:T(1,128)}...) custom-call(s32[2]{0:T(128)} %lengths_ref.3, f32[2,128,768]{2,1,0:T(8,128)} %inputs_ref.3, ...), custom_call_target="tpu_custom_call" | custom-call | tf_op jit(solution)/shard_map/feed_and_back/pallas_call | solution.py:1740
  155.2 2.7 %hand_over.1 = (f32[2,128,768]{2,1,0:T(8,128)}, f32[2,128,768]{2,1,0:T(8,128)}, f32[24,2304]{1,0:T(8,128)}, f32[24,768]{1,0:T(8,128)}, f32[8,24]{1,0:T(8,128)}, ...) custom-call(f32[2,128,768]{2,1,0:T(8,128)} %get-tuple-element.44.refs_0_, ...), custom_call_target="tpu_custom_call" | custom-call | tf_op jit(solution)/shard_map/hand_over/pallas_call | solution.py:1784

commit v3 on v2

--- a/solution.py
+++ b/solution.py
@@ -1767,12 +1767,27 @@
 
 def hand_over(*arrays):
     count = len(arrays)
+    pieces = []
+    for n, array in enumerate(arrays):
+        if array.ndim == 3:
+            half = array.shape[1] // 2
+            pieces += [
+                (n, (i, pl.ds(j * half, half))) for i in range(array.shape[0]) for j in range(2)
+            ]
+        else:
+            pieces.append((n, slice(None)))
 
     def body(*refs):
         came, out, held = refs[:count], refs[count : 2 * count], refs[2 * count : 3 * count]
         sems = refs[3 * count]
-        loads = [pltpu.make_async_copy(came[n], held[n], sems.at[0, n]) for n in range(count)]
-        stores = [pltpu.make_async_copy(held[n], out[n], sems.at[1, n]) for n in range(count)]
+        loads = [
+            pltpu.make_async_copy(came[n].at[cut], held[n].at[cut], sems.at[0, i])
+            for i, (n, cut) in enumerate(pieces)
+        ]
+        stores = [
+            pltpu.make_async_copy(held[n].at[cut], out[n].at[cut], sems.at[1, i])
+            for i, (n, cut) in enumerate(pieces)
+        ]
         for copy in loads:
             copy.start()
         for load, store in zip(loads, stores):
@@ -1786,7 +1801,7 @@
         out_shape=tuple(jax.ShapeDtypeStruct(a.shape, a.dtype) for a in arrays),
         in_specs=[ANY] * count,
         out_specs=(ANY,) * count,
-        scratch_shapes=[pltpu.VMEM(a.shape, a.dtype) for a in arrays] + [DMA((2, count))],
+        scratch_shapes=[pltpu.VMEM(a.shape, a.dtype) for a in arrays] + [DMA((2, len(pieces)))],
         name="hand_over",
         compiler_params=pltpu.CompilerParams(vmem_limit_bytes=VMEM_LIMIT),
     )(*arrays)

time: 158 us -> 158 us (level)
  no operation moved by 1% of the time
where the time goes in v3:
time: 158 us
  Pallas kernels  157 us (99%)
    pallas_call x1, Pallas kernels, feed_and_back(): pl.pallas_call(body, out_shape=tuple((jax.ShapeDtypeStruct(shape, F32) fo...  86.1 us
    pallas_call x1, Pallas kernels, gather_attend(): pl.pallas_call(body, out_shape=(jax.ShapeDtypeStruct((8, model_width), F3...  68.5 us

profile of v3, /device:TPU:0, one launch (start us, length us, event | category | flops | bytes accessed | tf_op | source)
XLA Modules:
  0.0 158.1 jit_solution(15505891985496626049)
XLA Ops:
  0.6 68.5 %gather_attend.1 = (f32[8,768]{1,0:T(8,128)}, f32[1,3072]{1,0:T(1,128)}, bf16[4,2,128,768]{3,2,1,0:T(8,128)(2,1)}, bf16[768,576]{1,0:T(8,128)(2,1)}, bf16[1024,5...) custom-call(s32[2]{0:T(128)} %lengths_ref.3, ...), custom_call_target="tpu_custom_call" | custom-call | tf_op jit(solution)/shard_map/gather_attend/pallas_call | solution.py:936
  69.1 86.1 %feed_and_back.1 = (f32[2,128,768]{2,1,0:T(8,128)}, f32[2,128,768]{2,1,0:T(8,128)}, f32[24,2304]{1,0:T(8,128)}, f32[8,24]{1,0:T(8,128)}, f32[1,96]{1,0:T(1,128)}...) custom-call(s32[2]{0:T(128)} %lengths_ref.3, f32[2,128,768]{2,1,0:T(8,128)} %inputs_ref.3, ...), custom_call_target="tpu_custom_call" | custom-call | tf_op jit(solution)/shard_map/feed_and_back/pallas_call | solution.py:1740
  155.2 2.7 %hand_over.1 = (f32[2,128,768]{2,1,0:T(8,128)}, f32[2,128,768]{2,1,0:T(8,128)}, f32[24,2304]{1,0:T(8,128)}, f32[24,768]{1,0:T(8,128)}, f32[8,24]{1,0:T(8,128)}, ...) custom-call(f32[2,128,768]{2,1,0:T(8,128)} %get-tuple-element.44.refs_0_, ...), custom_call_target="tpu_custom_call" | custom-call | tf_op jit(solution)/shard_map/hand_over/pallas_call | solution.py:1799

commit v4 on v2

--- a/solution.py
+++ b/solution.py
@@ -1357,7 +1357,7 @@
     def first(self):
         pos = self.pos
         self.sibling_copy().wait_recv()
-        for d in (*range(1, pos.nb), 0):
+        for d in (2, *(n for n in range(1, pos.nb) if n != 2), 0):
             z = pos.up(d)
             self.partial[z, :, pos.c] = (
                 self.partial[z, :, pos.c].astype(F32) + self.theirs[z].astype(F32)

time: 158 us -> 158 us (level)
  no operation moved by 1% of the time
where the time goes in v4:
time: 158 us
  Pallas kernels  157 us (99%)
    pallas_call x1, Pallas kernels, feed_and_back(): pl.pallas_call(body, out_shape=tuple((jax.ShapeDtypeStruct(shape, F32) fo...  86.1 us
    pallas_call x1, Pallas kernels, gather_attend(): pl.pallas_call(body, out_shape=(jax.ShapeDtypeStruct((8, model_width), F3...  68.5 us

profile of v4, /device:TPU:0, one launch (start us, length us, event | category | flops | bytes accessed | tf_op | source)
XLA Modules:
  0.0 158.1 jit_solution(7537998536214894696)
XLA Ops:
  0.6 68.5 %gather_attend.1 = (f32[8,768]{1,0:T(8,128)}, f32[1,3072]{1,0:T(1,128)}, bf16[4,2,128,768]{3,2,1,0:T(8,128)(2,1)}, bf16[768,576]{1,0:T(8,128)(2,1)}, bf16[1024,5...) custom-call(s32[2]{0:T(128)} %lengths_ref.3, ...), custom_call_target="tpu_custom_call" | custom-call | tf_op jit(solution)/shard_map/gather_attend/pallas_call | solution.py:936
  69.1 86.1 %feed_and_back.1 = (f32[2,128,768]{2,1,0:T(8,128)}, f32[2,128,768]{2,1,0:T(8,128)}, f32[24,2304]{1,0:T(8,128)}, f32[8,24]{1,0:T(8,128)}, f32[1,96]{1,0:T(1,128)}...) custom-call(s32[2]{0:T(128)} %lengths_ref.3, f32[2,128,768]{2,1,0:T(8,128)} %inputs_ref.3, ...), custom_call_target="tpu_custom_call" | custom-call | tf_op jit(solution)/shard_map/feed_and_back/pallas_call | solution.py:1740
  155.2 2.7 %hand_over.1 = (f32[2,128,768]{2,1,0:T(8,128)}, f32[2,128,768]{2,1,0:T(8,128)}, f32[24,2304]{1,0:T(8,128)}, f32[24,768]{1,0:T(8,128)}, f32[8,24]{1,0:T(8,128)}, ...) custom-call(f32[2,128,768]{2,1,0:T(8,128)} %get-tuple-element.44.refs_0_, ...), custom_call_target="tpu_custom_call" | custom-call | tf_op jit(solution)/shard_map/hand_over/pallas_call | solution.py:1784
